TPU v7x, 32 devices: a whole 2x2x4 slice. The times are simulated.
32 devices in a mesh: groups: 2 (over x), dp: 16 (over z, y, core).
Axes of the slice: x: 2, y: 2, z: 4, core: 2. Of those that a mesh axis runs over, the one named last changes fastest.
Arguments:
- hidden_input_rows: bfloat16 [8192, 8192], P(('groups', 'dp')), parts along dimension 0, may hold values from -6 to 6
- rank_cotangent: bfloat16 [8192, 128], P(('groups', 'dp')), parts along dimension 0, may hold values from -0.25 to 0.25
- token_identifiers: int32 [8192], P(('groups', 'dp')), parts along dimension 0, may hold values from 0 to 31999, as said below
- adam_first_moment: float32 [8192, 128], P('dp'), may hold values from -0.6 to 0.6
- adam_second_moment: float32 [8192, 128], P('dp'), may hold values from 0.0001 to 0.01
- block_seeds: int32 [8], replicated, may hold values from 0 to 1073741823
Outputs:
- feature_rows: float32 [32, 2048], P(('groups', 'dp')), parts along dimension 0
There are 2 independent parts, one for each index of `groups`. A program takes and returns all parts, laid end to end along the dimension named above; an argument that names none is the same for every part. Nothing has to cross between parts.
Inputs may be any that keep to these rules, and one draw needn't show every extreme that they name: `token_identifiers`: 0 marks padding. In each sequence of 512 positions the real tokens (ids 1 and up) come first and number at least 128; the rest is padding. Some sequence has no padding.
All inputs are finite; a program needn't handle non-finite values.
Results may differ from a plain program's by a relative error of at most 0.0029.
Values sent between devices are 32-bit elements; how exact they have to be, the bound alone decides.
No kernel may reach another device: no remote copies, remote signals or barrier semaphores. Data moves between devices by JAX's collectives and lax.ppermute only.
A program may use at most 64 MiB of HBM per device.

v0:
```python
import math

import jax
import jax.numpy as jnp
from jax import lax
from jax.sharding import PartitionSpec as P

FEAT_BLOCK = 512


beta_one = 0.9
beta_two = 0.999
epsilon = 1e-08
mix_feature = 1640531527
mix_param = 2028178513
mix_round = 73244475


def partner_2(value, axis, apart):
    mask = 2**apart
    pairs = [(source, source ^ mask) for source in range(lax.axis_size(axis))]
    return lax.ppermute(value, axis, pairs)


def scramble(hashed):
    hashed = hashed ^ lax.shift_right_logical(hashed, jnp.full_like(hashed, 16))
    hashed = hashed * mix_round
    hashed = hashed ^ lax.shift_right_logical(hashed, jnp.full_like(hashed, 16))
    hashed = hashed * mix_round
    hashed = hashed ^ lax.shift_right_logical(hashed, jnp.full_like(hashed, 16))
    return hashed


def sign_block(seed_values, feature_index, param_index):
    hashed = (
        seed_values[:, None]
        + feature_index[:, None] * mix_feature
        + param_index[None, :] * mix_param
    )
    hashed = scramble(hashed)
    return 1 - 2 * lax.shift_right_logical(hashed, jnp.full_like(hashed, 31))


def local(
    hidden_input_rows,
    rank_cotangent,
    token_identifiers,
    adam_first_moment,
    adam_second_moment,
    block_seeds,
):
    device_list = lax.axis_size("dp")
    my_index = lax.axis_index("dp")
    hidden_width = hidden_input_rows.shape[1]
    adapter_rank_size = rank_cotangent.shape[1]
    local_rows = adam_first_moment.shape[0]
    padding_mask = (token_identifiers != 0).astype(jnp.bfloat16)
    masked_values = rank_cotangent * padding_mask[:, None]
    half_gradient = lax.dot_general(
        hidden_input_rows,
        masked_values,
        (((0,), (0,)), ((), ())),
        preferred_element_type=jnp.float32,
    )
    block_list = half_gradient.reshape(device_list, local_rows, adapter_rank_size)
    half_rows = local_rows // 2
    split_blocks = block_list.reshape(device_list, 2, half_rows, adapter_rank_size)
    my_side = my_index % 2
    kept_rows = lax.dynamic_index_in_dim(split_blocks, my_side, 1, keepdims=False)
    given_rows = lax.dynamic_index_in_dim(split_blocks, 1 - my_side, 1, keepdims=False)
    partner = partner_2(given_rows, "dp", 0)
    summed = kept_rows + partner
    received_rows = lax.all_to_all(summed, "dp", split_axis=0, concat_axis=0, tiled=True)
    gradient = received_rows.reshape(device_list // 2, local_rows, adapter_rank_size)
    moment_one = beta_one * adam_first_moment[None] + (1 - beta_one) * gradient
    moment_two = beta_two * adam_second_moment[None] + (1 - beta_two) * gradient * gradient
    direction = (moment_one / (jnp.sqrt(moment_two) + epsilon)).astype(jnp.bfloat16)
    parameter_slice = local_rows * adapter_rank_size
    direction = direction.reshape(device_list // 2, parameter_slice)
    param_index = my_index * parameter_slice + jnp.arange(parameter_slice, dtype=jnp.int32)
    projection_scale = 1.0 / math.sqrt(hidden_width * adapter_rank_size)
    block_count = block_seeds.shape[0]

    def project(block_number, running):
        seed_value = lax.dynamic_index_in_dim(block_seeds, block_number, 0, keepdims=False)
        feature_index = block_number * FEAT_BLOCK + jnp.arange(FEAT_BLOCK, dtype=jnp.int32)
        seed_values = jnp.full((FEAT_BLOCK,), seed_value, jnp.int32)
        sign_tile = sign_block(seed_values, feature_index, param_index).astype(jnp.bfloat16)
        projected = lax.dot_general(
            direction, sign_tile, (((1,), (1,)), ((), ())), preferred_element_type=jnp.float32
        )
        return lax.dynamic_update_slice_in_dim(
            running, projected * projection_scale, block_number * FEAT_BLOCK, 1
        )

    partials = lax.fori_loop(
        jnp.int32(0),
        jnp.int32(block_count),
        project,
        jnp.zeros((device_list // 2, block_count * FEAT_BLOCK), jnp.float32),
    )
    partials = partials.reshape(device_list, block_count * FEAT_BLOCK // 2)
    return lax.psum_scatter(partials, "dp", scatter_dimension=0, tiled=True)


def solution(mesh):
    in_specs = (
        P(("groups", "dp"), None),
        P(("groups", "dp"), None),
        P(("groups", "dp")),
        P("dp", None),
        P("dp", None),
        P(),
    )
    out_specs = P(("groups", "dp"), None)
    return jax.shard_map(local, mesh=mesh, in_specs=in_specs, out_specs=out_specs, check_vma=False)
```

profile of v0, /device:TPU:0, one launch (start us, length us, event | category | flops | bytes accessed | tf_op | source)
XLA Modules:
  0.0 696.3 jit_solution(12888396023853559577)
XLA Ops:
  6.5 0.7 compare_convert_fusion
  7.2 5.0 convolution_bitcast_fusion
  12.2 6.6 reshape_reshape.3
  18.8 9.2 %constant_dynamic-slice_fusion.2 = (f32[16,1,256,128]{2,1,0,3:T(1,128)S(1)}, f32[16,1,256,128]{2,1,0,3:T(1,128)}) fusion(f32[16,2,256,128]{2,1,0,3:T(2,128)} %reshape_reshape.3, s32[]{:T(128)S(6)} %select_n.20, s32[]{:T(128)S(6)} %select_n.21), kind=kLoop, calls=%fused_computation.36 | loop fusion | bytes 8388616 | tf_op jit(solution)/shard_map/jit(dynamic_index_in_dim)/dynamic_slice | solution.py:69
  28.1 6.1 copy.12
  34.7 3.8 copy.11
  38.8 3.8 bitcast_add_fusion
  42.6 7.3 %all-to-all-start = ((f32[16,256,128]{2,1,0:T(8,128)}), f32[16,256,128]{2,1,0:T(8,128)}, u32[]{:S(2)}, u32[]{:S(2)}) async-start(f32[16,256,128]{2,1,0:T(8,128)} %bitcast_add_fusion), calls=%async_computation | async-start | bytes 4194304 | tf_op jit(solution)/shard_map/all_to_all | solution.py:73
  50.1 40.9 %all-to-all-done = f32[16,256,128]{2,1,0:T(8,128)} async-done(((f32[16,256,128]{2,1,0:T(8,128)}), f32[16,256,128]{2,1,0:T(8,128)}, u32[]{:S(2)}, u32[]{:S(2)}) %all-to-all-start) | async-done | bytes 2097184 | tf_op jit(solution)/shard_map/all_to_all | solution.py:73
  91.0 2.0 reshape.29
  93.0 2.0 fusion.28
  95.0 496.8 %while.11 = (s32[]{:T(128)}, f32[8,4096]{1,0:T(8,128)S(1)}, s32[8]{0:T(128)S(1)}, bf16[8,65536]{1,0:T(8,128)(2,1)}, s32[]{:T(128)}, /*index=5*/s32[]{:T(128)}, s32[]{:T(128)}, s32[]{:T(128)}, s32[]{:T(128)}) while((s32[]{:T(128)}, f32[8,4096]{1,0:T(8,128)S(1)}, s32[8]{0:T(128)S(1)}, bf16[8,65536]{1,0:T(8,128)(2,1)}, s32[]{:T(128)}, ...), condition=%wide.region_1.2_spmd.clone, body=%wide.region_0.1_spmd.clone.sunk | while | flops 973215232 | bytes 1593511 | solution.py:96
  95.8 0.6 multiply_add_fusion.2
  96.5 60.7 %fusion.41 = f32[8,4096]{1,0:T(8,128)S(1)} fusion(f32[8,4096]{1,0:T(8,128)S(1)} %get-tuple-element.101, s32[]{:T(128)S(6)} %select_n.24, bf16[8,65536]{1,0:T(8,128)(2,1)} %get-tuple-element.112, s32[65536]{0:T(1024)S(1)} %add_multiply_fusion.2, s32[512]{0:T(512)S(1)} %multiply_add_fusion.2), kind=kOutput, calls=%fused_computation.13.clone.2 | convolution fusion | flops 973082624 | bytes 1329156 | tf_op jit(solution)/shard_map/while/body/dot_general | solution.py:89
  157.3 0.6 dynamic_slice.17
  158.6 60.7 %fusion.41 = f32[8,4096]{1,0:T(8,128)S(1)} fusion(f32[8,4096]{1,0:T(8,128)S(1)} %get-tuple-element.101, s32[]{:T(128)S(6)} %select_n.24, bf16[8,65536]{1,0:T(8,128)(2,1)} %get-tuple-element.112, s32[65536]{0:T(1024)S(1)} %add_multiply_fusion.2, s32[512]{0:T(512)S(1)} %multiply_add_fusion.2), kind=kOutput, calls=%fused_computation.13.clone.2 | convolution fusion | flops 973082624 | bytes 1329156 | tf_op jit(solution)/shard_map/while/body/dot_general | solution.py:89
  219.4 0.6 dynamic_slice.17
  220.0 0.6 multiply_add_fusion.2
  220.7 60.7 %fusion.41 = f32[8,4096]{1,0:T(8,128)S(1)} fusion(f32[8,4096]{1,0:T(8,128)S(1)} %get-tuple-element.101, s32[]{:T(128)S(6)} %select_n.24, bf16[8,65536]{1,0:T(8,128)(2,1)} %get-tuple-element.112, s32[65536]{0:T(1024)S(1)} %add_multiply_fusion.2, s32[512]{0:T(512)S(1)} %multiply_add_fusion.2), kind=kOutput, calls=%fused_computation.13.clone.2 | convolution fusion | flops 973082624 | bytes 1329156 | tf_op jit(solution)/shard_map/while/body/dot_general | solution.py:89
  281.4 0.6 dynamic_slice.17
  282.8 60.7 %fusion.41 = f32[8,4096]{1,0:T(8,128)S(1)} fusion(f32[8,4096]{1,0:T(8,128)S(1)} %get-tuple-element.101, s32[]{:T(128)S(6)} %select_n.24, bf16[8,65536]{1,0:T(8,128)(2,1)} %get-tuple-element.112, s32[65536]{0:T(1024)S(1)} %add_multiply_fusion.2, s32[512]{0:T(512)S(1)} %multiply_add_fusion.2), kind=kOutput, calls=%fused_computation.13.clone.2 | convolution fusion | flops 973082624 | bytes 1329156 | tf_op jit(solution)/shard_map/while/body/dot_general | solution.py:89
  343.5 0.6 dynamic_slice.17
  344.8 60.7 %fusion.41 = f32[8,4096]{1,0:T(8,128)S(1)} fusion(f32[8,4096]{1,0:T(8,128)S(1)} %get-tuple-element.101, s32[]{:T(128)S(6)} %select_n.24, bf16[8,65536]{1,0:T(8,128)(2,1)} %get-tuple-element.112, s32[65536]{0:T(1024)S(1)} %add_multiply_fusion.2, s32[512]{0:T(512)S(1)} %multiply_add_fusion.2), kind=kOutput, calls=%fused_computation.13.clone.2 | convolution fusion | flops 973082624 | bytes 1329156 | tf_op jit(solution)/shard_map/while/body/dot_general | solution.py:89
  405.6 0.6 dynamic_slice.17
  406.9 60.7 %fusion.41 = f32[8,4096]{1,0:T(8,128)S(1)} fusion(f32[8,4096]{1,0:T(8,128)S(1)} %get-tuple-element.101, s32[]{:T(128)S(6)} %select_n.24, bf16[8,65536]{1,0:T(8,128)(2,1)} %get-tuple-element.112, s32[65536]{0:T(1024)S(1)} %add_multiply_fusion.2, s32[512]{0:T(512)S(1)} %multiply_add_fusion.2), kind=kOutput, calls=%fused_computation.13.clone.2 | convolution fusion | flops 973082624 | bytes 1329156 | tf_op jit(solution)/shard_map/while/body/dot_general | solution.py:89
  467.7 0.6 dynamic_slice.17
  469.0 60.7 %fusion.41 = f32[8,4096]{1,0:T(8,128)S(1)} fusion(f32[8,4096]{1,0:T(8,128)S(1)} %get-tuple-element.101, s32[]{:T(128)S(6)} %select_n.24, bf16[8,65536]{1,0:T(8,128)(2,1)} %get-tuple-element.112, s32[65536]{0:T(1024)S(1)} %add_multiply_fusion.2, s32[512]{0:T(512)S(1)} %multiply_add_fusion.2), kind=kOutput, calls=%fused_computation.13.clone.2 | convolution fusion | flops 973082624 | bytes 1329156 | tf_op jit(solution)/shard_map/while/body/dot_general | solution.py:89
  529.7 0.6 dynamic_slice.17
  531.1 60.7 %fusion.41 = f32[8,4096]{1,0:T(8,128)S(1)} fusion(f32[8,4096]{1,0:T(8,128)S(1)} %get-tuple-element.101, s32[]{:T(128)S(6)} %select_n.24, bf16[8,65536]{1,0:T(8,128)(2,1)} %get-tuple-element.112, s32[65536]{0:T(1024)S(1)} %add_multiply_fusion.2, s32[512]{0:T(512)S(1)} %multiply_add_fusion.2), kind=kOutput, calls=%fused_computation.13.clone.2 | convolution fusion | flops 973082624 | bytes 1329156 | tf_op jit(solution)/shard_map/while/body/dot_general | solution.py:89
  591.8 0.7 reshape.30
  593.2 94.3 %all-reduce.3.cloned.1.call-done = f32[16,2048]{1,0:T(8,128)} async-done(((f32[16,2048]{1,0:T(8,128)}), f32[16,2048]{1,0:T(8,128)}) %all-reduce.3.cloned.1.call-update) | async-done | bytes 131088
  687.5 2.0 constant_dynamic-slice_fusion
  (30 shorter events, 6.2 us)
Async XLA Ops:
  34.2 4.6 collective-permute-start
  38.5 11.5 %copy-start = (f32[512,128]{1,0:T(8,128)S(1)}, f32[512,128]{1,0:T(8,128)}, u32[]{:S(2)}) copy-start(f32[512,128]{1,0:T(8,128)} %param.12) | copy-start | bytes 786436
  38.5 11.5 %copy-start.1 = (f32[512,128]{1,0:T(8,128)S(1)}, f32[512,128]{1,0:T(8,128)}, u32[]{:S(2)}) copy-start(f32[512,128]{1,0:T(8,128)} %param.11) | copy-start | bytes 786436
  42.6 48.4 %all-to-all-start = ((f32[16,256,128]{2,1,0:T(8,128)}), f32[16,256,128]{2,1,0:T(8,128)}, u32[]{:S(2)}, u32[]{:S(2)}) async-start(f32[16,256,128]{2,1,0:T(8,128)} %bitcast_add_fusion), calls=%async_computation | async-start | bytes 4194304 | tf_op jit(solution)/shard_map/all_to_all | solution.py:73
  50.0 637.5 %all-reduce.3.cloned.1.call-start = ((), (), s32[]{:S(2)}) async-start(), calls=%async_computation.1 | async-start | bytes 262144
  50.1 44.9 %copy-start.2 = (s32[8]{0:T(128)S(1)}, s32[8]{0:T(128)}, u32[]{:S(2)}) copy-start(s32[8]{0:T(128)} %param.13) | copy-start | bytes 100
  95.0 497.6 %copy-start.3 = (u32[32]{0:T(128)S(1)}, u32[32]{0:T(128)}, u32[]{:S(2)}) copy-start(u32[32]{0:T(128)} %constant.74) | copy-start | bytes 388
Sparse Core Ops, SparseCore 0:
  592.7 94.7 all-reduce.2
where the time goes:
time: 698 us; the launch traced here: 696 us
  matrix products  491 us (70%)
  waiting for transfers between devices  136 us (19%)
  local copies, waits for them, and re-layouts  36.2 us (5%)
  between operations  13.5 us (2%)
  other arithmetic  11.9 us (2%)
  starting transfers between devices  7.88 us (1%)
    dot_general x8, matrix products, project(): lax.dot_general(direction, sign_tile, (((1,), (1,)), ((), ())), preferred...  486 us
    unnamed x2, waiting for transfers between devices  94.3 us
    all_to_all x1, waiting for transfers between devices, local(): lax.all_to_all(summed, 'dp', split_axis=0, concat_axis=0, tiled=True)  40.9 us
  transfers between devices with their start and end apart: 3, of which 3 were waited for; matrix products, arithmetic and copies ran while one was open for 1% of the time, Pallas kernels for 0%

commit v1 on v0

v1 whole, which is shorter than its diff:
```python
import functools
import math

import jax
import jax.numpy as jnp
from jax import lax
from jax.experimental import pallas as pl
from jax.experimental.pallas import tpu as pltpu
from jax.sharding import PartitionSpec as P

FEAT_BLOCK = 512
beta_one = 0.9
beta_two = 0.999
epsilon = 1e-08
mix_feature = 1640531527
mix_param = 2028178513
mix_round = 73244475
DIGITS = 4
RADIX = 16.0
FP8 = jnp.float8_e4m3fn
STEP_ROWS = 2048
KEPT_ROWS = 512
TILE_ROWS = 512
TILE_FEATS = 2048


def wrap(value):
    value &= 0xFFFFFFFF
    return jnp.int32(value - (1 << 32) if value >= (1 << 31) else value)


def scramble(hashed):
    hashed = hashed ^ lax.shift_right_logical(hashed, jnp.full_like(hashed, 16))
    hashed = hashed * mix_round
    hashed = hashed ^ lax.shift_right_logical(hashed, jnp.full_like(hashed, 16))
    return hashed * mix_round


def first_param(rows, groups, rank):
    mine = lax.axis_index("dp") * groups + lax.axis_index("groups")
    return mine * (rows * rank)


def hash_base(seed_ref, feature_tile, start):
    pieces = []
    for piece in range(TILE_FEATS // FEAT_BLOCK):
        block = feature_tile * (TILE_FEATS // FEAT_BLOCK) + piece
        down = lax.broadcasted_iota(jnp.int32, (8, FEAT_BLOCK), 0)
        across = lax.broadcasted_iota(jnp.int32, (8, FEAT_BLOCK), 1)
        scalar = seed_ref[block] + block * wrap(FEAT_BLOCK * mix_feature) + start * wrap(mix_param)
        pieces.append(down * wrap(mix_param) + across * wrap(mix_feature) + scalar)
    return jnp.concatenate(pieces, axis=1)


def write_signs(base, rows, out_ref):
    for top in range(0, rows, 32):
        hashes = [scramble(base + wrap(mix_param * (top + 8 * part))) for part in range(4)]
        hashed = jnp.concatenate(hashes, axis=0)
        out_ref[pl.ds(top, 32), :] = jnp.where(hashed < 0, FP8(-1), FP8(1))


def gradient_kernel(side_ref, inputs_ref, masked_ref, out_ref):
    out_ref[0] = lax.dot_general(
        inputs_ref[...],
        masked_ref[...],
        (((0,), (0,)), ((), ())),
        preferred_element_type=jnp.float32,
    )


def gradient_sum_kernel(side_ref, inputs_ref, masked_ref, other_ref, out_ref):
    out_ref[0] = other_ref[0] + lax.dot_general(
        inputs_ref[...],
        masked_ref[...],
        (((0,), (0,)), ((), ())),
        preferred_element_type=jnp.float32,
    )


def half_gradient(inputs, masked, side, groups, rows, other=None):
    tokens, width = inputs.shape
    rank = masked.shape[1]
    pairs = width // (2 * groups * rows)
    shape = (groups * pairs, rows, rank)
    if rows % 128:
        whole = lax.dot_general(
            inputs, masked, (((0,), (0,)), ((), ())), preferred_element_type=jnp.float32
        )
        whole = whole.reshape(pairs, 2, groups, rows, rank)
        mine = lax.dynamic_index_in_dim(whole, side, 1, keepdims=False).swapaxes(0, 1).reshape(shape)
        return mine if other is None else mine + other
    block_map = lambda pair, group, side_ref: (group * pairs + pair, 0, 0)
    in_specs = [
        pl.BlockSpec(
            (tokens, rows), lambda pair, group, side_ref: (0, (2 * pair + side_ref[0]) * groups + group)
        ),
        pl.BlockSpec((tokens, rank), lambda pair, group, side_ref: (0, 0)),
    ]
    operands = [inputs, masked]
    if other is not None:
        in_specs.append(pl.BlockSpec((1, rows, rank), block_map))
        operands.append(other)
    return pl.pallas_call(
        gradient_kernel if other is None else gradient_sum_kernel,
        grid_spec=pltpu.PrefetchScalarGridSpec(
            num_scalar_prefetch=1,
            grid=(pairs, groups),
            in_specs=in_specs,
            out_specs=pl.BlockSpec((1, rows, rank), block_map),
        ),
        out_shape=jax.ShapeDtypeStruct(shape, jnp.float32),
        cost_estimate=pl.CostEstimate(
            flops=tokens * width * rank, bytes_accessed=tokens * width + 4 * width * rank, transcendentals=0
        ),
        name="half_gradient",
    )(side[None], *operands)


def signs_kernel(rows, groups, rank, seed_ref, out_ref):
    start = first_param(rows, groups, rank) + pl.program_id(0) * STEP_ROWS
    write_signs(hash_base(seed_ref, pl.program_id(1), start), KEPT_ROWS, out_ref)


def kept_signs(seeds, rows, groups, rank):
    steps = rows * rank // STEP_ROWS
    features = seeds.shape[0] * FEAT_BLOCK
    total = steps * KEPT_ROWS * features
    return pl.pallas_call(
        functools.partial(signs_kernel, rows, groups, rank),
        grid=(steps, features // TILE_FEATS),
        in_specs=[pl.BlockSpec(memory_space=pltpu.SMEM)],
        out_specs=pl.BlockSpec((KEPT_ROWS, TILE_FEATS), lambda step, tile: (step, tile)),
        out_shape=jax.ShapeDtypeStruct((steps * KEPT_ROWS, features), FP8),
        cost_estimate=pl.CostEstimate(flops=total * 10, bytes_accessed=total, transcendentals=0),
        name="kept_signs",
    )(seeds)


def direction_kernel(rows, gradient_ref, first_ref, second_ref, out_ref, scale_ref, held):
    sequences, rank = gradient_ref.shape[0], gradient_ref.shape[2]
    start = lax.axis_index("groups") * rows

    def moments(block, largest):
        at = pl.ds(pl.multiple_of(block * 8, 8), 8)
        here = pl.ds(pl.multiple_of(start + block * 8, 8), 8)
        gradient = gradient_ref[:, at, :]
        moment_one = beta_one * first_ref[here, :][None] + (1 - beta_one) * gradient
        moment_two = beta_two * second_ref[here, :][None] + (1 - beta_two) * gradient * gradient
        direction = moment_one / (jnp.sqrt(moment_two) + epsilon)
        direction = direction.astype(jnp.bfloat16).astype(jnp.float32)
        direction = jnp.swapaxes(direction, 0, 1)
        for row in range(8):
            held[block * 8 + row] = direction[row]
        return jnp.maximum(largest, jnp.max(jnp.abs(direction), axis=0))

    largest = lax.fori_loop(0, rows // 8, moments, jnp.zeros((sequences, rank), jnp.float32))
    largest = jnp.broadcast_to(jnp.max(largest, axis=1, keepdims=True), (sequences, rank))
    scale = jnp.ones_like(largest)
    for power in (64, 32, 16, 8, 4, 2, 1):
        room = largest * (2.0**power) < RADIX
        largest = jnp.where(room, largest * (2.0**power), largest)
        scale = jnp.where(room, scale * (2.0**power), scale)
    for power in (2, 1):
        over = largest >= RADIX
        largest = jnp.where(over, largest * (0.5**power), largest)
        scale = jnp.where(over, scale * (0.5**power), scale)
    scale_ref[...] = scale

    def split(row, _):
        rest = held[row] * scale
        digits = []
        for _ in range(DIGITS):
            digit = jnp.round(rest)
            digits.append(digit)
            rest = (rest - digit) * RADIX
        out_ref[:, pl.ds(pl.multiple_of(row * rank, rank), rank)] = jnp.concatenate(digits, axis=0).astype(FP8)
        return 0

    lax.fori_loop(0, rows, split, 0, unroll=8)


def scaled_direction(gradient, first, second, rows):
    sequences, _, rank = gradient.shape
    return pl.pallas_call(
        functools.partial(direction_kernel, rows),
        out_shape=(
            jax.ShapeDtypeStruct((DIGITS * sequences, rows * rank), FP8),
            jax.ShapeDtypeStruct((sequences, rank), jnp.float32),
        ),
        scratch_shapes=[pltpu.VMEM((rows, sequences, rank), jnp.float32)],
        compiler_params=pltpu.CompilerParams(vmem_limit_bytes=48 << 20),
        cost_estimate=pl.CostEstimate(
            flops=20 * gradient.size, bytes_accessed=5 * gradient.size, transcendentals=2 * gradient.size
        ),
        name="direction",
    )(gradient, first, second)


def project_kernel(rows, groups, rank, final_scale, seed_ref, direction_ref, scale_ref, kept_ref, out_ref, total, *tiles):
    tile, step = pl.program_id(0), pl.program_id(1)
    sequences = scale_ref.shape[0]
    start = first_param(rows, groups, rank) + step * STEP_ROWS
    count = len(tiles)

    def multiply(at, signs):
        at = pl.multiple_of(at, TILE_ROWS)
        total[...] += jnp.dot(
            direction_ref[:, pl.ds(at, signs.shape[0])], signs[...], preferred_element_type=jnp.float32
        )

    @pl.when(step == 0)
    def _():
        total[...] = jnp.zeros_like(total)
        tiles[-1][...] = jnp.zeros_like(tiles[-1])

    here = step * STEP_ROWS
    for index in range(count):
        offset = KEPT_ROWS + index * TILE_ROWS
        write_signs(hash_base(seed_ref, tile, start + offset), TILE_ROWS, tiles[index])
        if index == 0:
            multiply(jnp.maximum(here - TILE_ROWS, 0), tiles[-1])
            multiply(here, kept_ref)
        else:
            multiply(here + offset - TILE_ROWS, tiles[index - 1])

    @pl.when(step == pl.num_programs(1) - 1)
    def _():
        multiply(here + STEP_ROWS - TILE_ROWS, tiles[-1])
        inverse = (1.0 / scale_ref[...])[:, :1]
        value = total[(DIGITS - 1) * sequences :, :]
        for digit in reversed(range(DIGITS - 1)):
            value = total[digit * sequences : (digit + 1) * sequences, :] + value * (1.0 / RADIX)
        out_ref[...] = value * inverse * final_scale


def project(seeds, direction, scale, kept, rows, groups, rank, final_scale):
    features = seeds.shape[0] * FEAT_BLOCK
    sequences = scale.shape[0]
    params = rows * rank
    steps = params // STEP_ROWS
    count = (STEP_ROWS - KEPT_ROWS) // TILE_ROWS
    return pl.pallas_call(
        functools.partial(project_kernel, rows, groups, rank, final_scale),
        grid=(features // TILE_FEATS, steps),
        in_specs=[
            pl.BlockSpec(memory_space=pltpu.SMEM),
            pl.BlockSpec((DIGITS * sequences, params), lambda tile, step: (0, 0)),
            pl.BlockSpec((sequences, rank), lambda tile, step: (0, 0)),
            pl.BlockSpec((KEPT_ROWS, TILE_FEATS), lambda tile, step: (step, tile)),
        ],
        out_specs=pl.BlockSpec((sequences, TILE_FEATS), lambda tile, step: (0, tile)),
        out_shape=jax.ShapeDtypeStruct((sequences, features), jnp.float32),
        scratch_shapes=[pltpu.VMEM((DIGITS * sequences, TILE_FEATS), jnp.float32)]
        + [pltpu.VMEM((TILE_ROWS, TILE_FEATS), FP8)] * count,
        cost_estimate=pl.CostEstimate(
            flops=10 * params * features, bytes_accessed=params * features // 4, transcendentals=0
        ),
        name="project",
    )(seeds, direction, scale, kept)


def local(
    hidden_input_rows,
    rank_cotangent,
    token_identifiers,
    adam_first_moment,
    adam_second_moment,
    block_seeds,
):
    groups, device_list = lax.axis_size("groups"), lax.axis_size("dp")
    hidden_width = hidden_input_rows.shape[1]
    rank = rank_cotangent.shape[1]
    rows = adam_first_moment.shape[0] // groups
    features = block_seeds.shape[0] * FEAT_BLOCK
    core = lax.axis_index("dp") & 1
    padding_mask = (token_identifiers != 0).astype(jnp.bfloat16)
    masked = rank_cotangent * padding_mask[:, None]

    given = half_gradient(hidden_input_rows, masked, 1 - core, groups, rows)
    pairs = [(source, source ^ 1) for source in range(device_list)]
    other = lax.ppermute(given, "dp", pairs)
    summed = half_gradient(hidden_input_rows, masked, core, groups, rows, other)
    kept = kept_signs(block_seeds, rows, groups, rank)

    half = device_list // 2
    everyone = [
        [group * device_list + 2 * pair + side for group in range(groups) for pair in range(half)]
        for side in range(2)
    ]
    gradient = lax.all_to_all(
        summed, ("groups", "dp"), split_axis=0, concat_axis=0, axis_index_groups=everyone, tiled=True
    )
    direction, scale = scaled_direction(gradient, adam_first_moment, adam_second_moment, rows)
    final_scale = 1.0 / math.sqrt(hidden_width * rank)
    partial = project(block_seeds, direction, scale, kept, rows, groups, rank, final_scale)
    partial = partial.reshape(groups * device_list, features // 2)
    partial = lax.all_to_all(partial, ("groups", "dp"), split_axis=0, concat_axis=0, tiled=True)
    return jnp.sum(partial, axis=0, keepdims=True)


def solution(mesh):
    in_specs = (
        P(("groups", "dp"), None),
        P(("groups", "dp"), None),
        P(("groups", "dp")),
        P("dp", None),
        P("dp", None),
        P(),
    )
    out_specs = P(("groups", "dp"), None)
    return jax.shard_map(local, mesh=mesh, in_specs=in_specs, out_specs=out_specs, check_vma=False)
```

time: 698 us -> 225 us (0.32)
  matrix products: 491 us -> 0 us
  Pallas kernels: 0 us -> 181 us
  waiting for transfers between devices: 136 us -> 12.3 us
  local copies, waits for them, and re-layouts: 36.2 us -> 4.57 us
  blocking collectives: 0 us -> 14.3 us
  between operations: 13.5 us -> 0.05 us
  other arithmetic: 11.9 us -> 3.01 us
    dot_general x9 -> x0, matrix products: 491 us -> none  [the longest x8 486 us: project(): lax.dot_general(direction, sign_tile, (((1,), (1,)), ((), ())), preferred...]
    pallas_call x0 -> x5, Pallas kernels: none -> 181 us  [the longest x1 117 us: project(): pl.pallas_call(functools.partial(project_kernel, rows, groups, rank, fina...]
    unnamed x2 -> x0, waiting for transfers between devices: 94.3 us -> none
    all_to_all x1, waiting for transfers between devices: 40.9 us -> 8.33 us  [local(): lax.all_to_all(summed, ('groups', 'dp'), split_axis=0, concat_axis=0, axi...]
    dynamic_slice x9 -> x0, local copies, waits for them, and re-layouts: 14.3 us -> none  [the longest x1 9.24 us: local(): lax.dynamic_index_in_dim(split_blocks, my_side, 1, keepdims=False)]
    all_to_all x0 -> x1, blocking collectives: none -> 14.3 us  [local(): lax.all_to_all(partial, ('groups', 'dp'), split_axis=0, concat_axis=0, ti...]
    unnamed x12 -> x10, local copies, waits for them, and re-layouts: 12.6 us -> 3.3 us
    add x10 -> x0, other arithmetic: 8.95 us -> none  [the longest x8 5.09 us: sign_block(): seed_values[:, None] + feature_index[:, None] * mix_feature]
  transfers between devices with their start and end apart: 3 -> 2, of which waited for: 3 -> 2; matrix products, arithmetic and copies ran while one was open for 1% -> 0% of each run, Pallas kernels for 0% -> 17%
where the time goes in v1:
time: 225 us; the launch traced here: 224 us
  Pallas kernels  181 us (80%)
  blocking collectives  14.3 us (6%)
  waiting for transfers between devices  12.3 us (5%)
  starting transfers between devices  8.71 us (4%)
  local copies, waits for them, and re-layouts  4.57 us (2%)
  other arithmetic  3.01 us (1%)
    pallas_call x1, Pallas kernels, project(): pl.pallas_call(functools.partial(project_kernel, rows, groups, rank, fina...  117 us
    pallas_call x1, Pallas kernels, kept_signs(): pl.pallas_call(functools.partial(signs_kernel, rows, groups, rank), grid=...  39.1 us
    pallas_call x2, Pallas kernels, half_gradient(): pl.pallas_call(gradient_kernel if other is None else gradient_sum_kernel,...  22.3 us
    all_to_all x1, blocking collectives, local(): lax.all_to_all(partial, ('groups', 'dp'), split_axis=0, concat_axis=0, ti...  14.3 us
    all_to_all x1, waiting for transfers between devices, local(): lax.all_to_all(summed, ('groups', 'dp'), split_axis=0, concat_axis=0, axi...  8.33 us
    all_to_all x1, starting transfers between devices, local(): lax.all_to_all(summed, ('groups', 'dp'), split_axis=0, concat_axis=0, axi...  8.22 us
  transfers between devices with their start and end apart: 2, of which 2 were waited for; matrix products, arithmetic and copies ran while one was open for 0% of the time, Pallas kernels for 17%

profile of v1, /device:TPU:0, one launch (start us, length us, event | category | flops | bytes accessed | tf_op | source)
XLA Modules:
  0.0 224.3 jit_solution(172308602624334162)
XLA Ops:
  0.0 0.7 compare_convert_fusion
  0.7 1.6 broadcast_multiply_fusion.masked_ref
  2.2 10.9 %half_gradient.2 = f32[16,256,128]{2,1,0:T(8,128)} custom-call(s32[1]{0:T(128)} %bitcast.1.side_ref, bf16[256,8192]{1,0:T(8,128)(2,1)} %inputs_ref.3, bf16[256,128]{1,0:T(8,128)(2,1)} %broadcast_multiply_fusion.masked_ref), custom_call_target="tpu_custom_call" | custom-call | flops 268435456 | bytes 6291456 | tf_op jit(solution)/shard_map/half_gradient/pallas_call | solution.py:103
  13.1 0.5 collective-permute-start
  13.6 4.0 %collective-permute-done.other_ref = f32[16,256,128]{2,1,0:T(8,128)S(1)} collective-permute-done((f32[16,256,128]{2,1,0:T(8,128)}, f32[16,256,128]{2,1,0:T(8,128)S(1)}, u32[]{:S(2)}, u32[]{:S(2)}) %collective-permute-start) | collective-permute-done | bytes 2097184 | tf_op jit(solution)/shard_map/ppermute | solution.py:281
  17.6 0.0 copy-start.4
  17.6 1.4 copy-done.4
  19.0 11.5 %half_gradient.3 = f32[16,256,128]{2,1,0:T(8,128)} custom-call(s32[1]{0:T(128)} %bitcast.side_ref, bf16[256,8192]{1,0:T(8,128)(2,1)} %inputs_ref.3, bf16[256,128]{1,0:T(8,128)(2,1)} %broadcast_multiply_fusion.masked_ref, f32[16,256,128]{2,1,0:T(8,128)} %copy-done.4), custom_call_target="tpu_custom_call" | custom-call | flops 268435456 | bytes 6291456 | tf_op jit(solution)/shard_map/half_gradient/pallas_call | solution.py:103
  30.4 8.2 %all-to-all-start = ((f32[16,256,128]{2,1,0:T(8,128)}), f32[16,256,128]{2,1,0:T(8,128)S(1)}, u32[]{:S(2)}, u32[]{:S(2)}) async-start(f32[16,256,128]{2,1,0:T(8,128)} %half_gradient.3), calls=%async_computation | async-start | bytes 4194304 | tf_op jit(solution)/shard_map/all_to_all | solution.py:290
  38.6 0.0 copy-start.1
  38.7 0.0 copy-start.2
  38.7 39.1 %kept_signs.1.kept_ref = f8e4m3fn[8192,4096]{1,0:T(32,128)(4,1)} custom-call(s32[8]{0:T(128)} %seed_ref.3), custom_call_target="tpu_custom_call" | custom-call | flops 335544320 | bytes 33554432 | tf_op jit(solution)/shard_map/kept_signs/pallas_call | solution.py:128
  77.8 8.3 %all-to-all-done.gradient_ref = f32[16,256,128]{2,1,0:T(8,128)S(1)} async-done(((f32[16,256,128]{2,1,0:T(8,128)}), f32[16,256,128]{2,1,0:T(8,128)S(1)}, u32[]{:S(2)}, u32[]{:S(2)}) %all-to-all-start) | async-done | bytes 2097184 | tf_op jit(solution)/shard_map/all_to_all | solution.py:290
  86.1 0.0 copy-done.1
  86.1 0.0 copy-done.2
  86.1 3.2 %direction.1 = (f8e4m3fn[64,32768]{1,0:T(32,128)(4,1)S(1)}, f32[16,128]{1,0:T(8,128)S(1)}) custom-call(f32[16,256,128]{2,1,0:T(8,128)S(1)} %all-to-all-done.gradient_ref, f32[512,128]{1,0:T(8,128)S(1)} %copy-done.1, f32[512,128]{1,0:T(8,128)S(1)} %copy-done.2), custom_call_target="tpu_custom_call" | custom-call | flops 10485760 | bytes 2621440 | tf_op jit(solution)/shard_map/direction/pallas_call | solution.py:184
  89.4 0.0 copy-start
  89.4 1.3 copy-done
  90.7 0.0 copy-start.3
  90.7 0.6 copy-done.3
  91.3 116.7 %project.1 = f32[16,4096]{1,0:T(8,128)} custom-call(s32[8]{0:T(128)} %seed_ref.3, f8e4m3fn[64,32768]{1,0:T(32,128)(4,1)} %copy-done, f32[16,128]{1,0:T(8,128)} %copy-done.3, f8e4m3fn[8192,4096]{1,0:T(32,128)(4,1)} %kept_signs.1.kept_ref), custom_call_target="tpu_custom_call" | custom-call | flops 1342177280 | bytes 33554432 | tf_op jit(solution)/shard_map/project/pallas_call | solution.py:242
  208.0 1.3 all_to_all.12
  209.3 14.3 %all_to_all.15 = f32[32,1,2048]{2,1,0:T(1,128)S(1)} all-to-all(f32[32,1,2048]{2,1,0:T(1,128)S(1)} %all_to_all.12), channel_id=1, replica_groups=mesh['groups'=2,'dp'=16] {'groups','dp'}, dimensions={0} | all-to-all | bytes 524288 | tf_op jit(solution)/shard_map/all_to_all | solution.py:297
  223.6 0.8 reduce_sum.9
Async XLA Ops:
  13.1 4.5 %collective-permute-start = (f32[16,256,128]{2,1,0:T(8,128)}, f32[16,256,128]{2,1,0:T(8,128)S(1)}, u32[]{:S(2)}, u32[]{:S(2)}) collective-permute-start(f32[16,256,128]{2,1,0:T(8,128)} %half_gradient.2), channel_id=1, source_target_pairs={{0,1},{1,0},{2,3},{3,2},{4,5},{5,4},{6,7},{7,6},{8,9},{9,8},{10,11... | collective-permute-start | bytes 6291464 | tf_op jit(solution)/shard_map/ppermute | solution.py:281
  17.6 1.4 copy-start.4
  30.4 55.7 %all-to-all-start = ((f32[16,256,128]{2,1,0:T(8,128)}), f32[16,256,128]{2,1,0:T(8,128)S(1)}, u32[]{:S(2)}, u32[]{:S(2)}) async-start(f32[16,256,128]{2,1,0:T(8,128)} %half_gradient.3), calls=%async_computation | async-start | bytes 4194304 | tf_op jit(solution)/shard_map/all_to_all | solution.py:290
  38.6 47.5 %copy-start.1 = (f32[512,128]{1,0:T(8,128)S(1)}, f32[512,128]{1,0:T(8,128)}, u32[]{:S(2)}) copy-start(f32[512,128]{1,0:T(8,128)} %first_ref.1) | copy-start | bytes 786436
  38.7 47.5 %copy-start.2 = (f32[512,128]{1,0:T(8,128)S(1)}, f32[512,128]{1,0:T(8,128)}, u32[]{:S(2)}) copy-start(f32[512,128]{1,0:T(8,128)} %second_ref.1) | copy-start | bytes 786436
  89.4 1.3 copy-start
  90.7 0.6 copy-start.3

commit v2 on v1

v2 whole, which is shorter than its diff:
```python
import functools
import math

import jax
import jax.numpy as jnp
from jax import lax
from jax.experimental import pallas as pl
from jax.experimental.pallas import tpu as pltpu
from jax.sharding import PartitionSpec as P

FEAT_BLOCK = 512
beta_one = 0.9
beta_two = 0.999
epsilon = 1e-08
mix_feature = 1640531527
mix_param = 2028178513
mix_round = 73244475
DIGITS = 4
RADIX = 16.0
FP8 = jnp.float8_e4m3fn
STEP_ROWS = 4096
KEPT_ROWS = 1280
TILES = (768, 768, 768, 512)
EARLY_BLOCKS = 2
TILE_FEATS = 2048


def wrap(value):
    value &= 0xFFFFFFFF
    return jnp.int32(value - (1 << 32) if value >= (1 << 31) else value)


def scramble(hashed):
    hashed = hashed ^ lax.shift_right_logical(hashed, jnp.full_like(hashed, 16))
    hashed = hashed * mix_round
    hashed = hashed ^ lax.shift_right_logical(hashed, jnp.full_like(hashed, 16))
    return hashed * mix_round


def strides(rows, rank):
    return (1, rank) if rows % 128 == 0 else (rank, 1)


def minor_size(rows, rank):
    return rows if rows % 128 == 0 else rank


def step_start(rows, rank, groups, step):
    mine = lax.axis_index("dp") * groups + lax.axis_index("groups")
    return mine * (rows * rank) + step * (STEP_ROWS // minor_size(rows, rank) * strides(rows, rank)[0])


def hash_base(seed_ref, feature_tile, start, minor_stride):
    pieces = []
    for piece in range(TILE_FEATS // FEAT_BLOCK):
        block = feature_tile * (TILE_FEATS // FEAT_BLOCK) + piece
        down = lax.broadcasted_iota(jnp.int32, (8, FEAT_BLOCK), 0)
        across = lax.broadcasted_iota(jnp.int32, (8, FEAT_BLOCK), 1)
        scalar = seed_ref[block] + block * wrap(FEAT_BLOCK * mix_feature) + start * wrap(mix_param)
        pieces.append(down * wrap(mix_param * minor_stride) + across * wrap(mix_feature) + scalar)
    return jnp.concatenate(pieces, axis=1)


def write_signs(base, rows, rank, offset, count, out_ref):
    minor, (major_stride, minor_stride) = minor_size(rows, rank), strides(rows, rank)
    for top in range(0, count, 32):
        hashes = []
        for part in range(offset + top, offset + top + 32, 8):
            apart = part // minor * major_stride + part % minor * minor_stride
            hashes.append(scramble(base + wrap(mix_param * apart)))
        hashed = jnp.concatenate(hashes, axis=0)
        out_ref[pl.ds(top, 32), :] = jnp.where(hashed < 0, FP8(-1), FP8(1))


def gradient_kernel(side_ref, inputs_ref, cotangent_ref, tokens_ref, *refs):
    *other_refs, out_ref, masked = refs
    other_refs = other_refs[:1]

    @pl.when(pl.program_id(0) == 0)
    def _():
        turned = cotangent_ref[...].astype(jnp.float32).T
        masked[...] = jnp.where(tokens_ref[...] != 0, turned, 0.0).astype(jnp.bfloat16)

    part = jnp.dot(masked[...], inputs_ref[...], preferred_element_type=jnp.float32)
    groups, rows = out_ref.shape[0], out_ref.shape[3]
    for group in range(groups):
        piece = part[:, group * rows : (group + 1) * rows]
        for other_ref in other_refs:
            piece = piece + other_ref[group, 0]
        out_ref[group, 0] = piece


def half_gradient(inputs, cotangent, tokens, side, groups, rows, other=None, after=None):
    count, width = inputs.shape
    rank = cotangent.shape[1]
    pairs = width // (2 * groups * rows)
    if rows % 128:
        masked = jnp.where((tokens != 0)[:, None], cotangent, jnp.bfloat16(0))
        whole = lax.dot_general(
            inputs, masked, (((0,), (0,)), ((), ())), preferred_element_type=jnp.float32
        )
        whole = whole.reshape(pairs, 2, groups, rows, rank)
        mine = lax.dynamic_index_in_dim(whole, side, 1, keepdims=False).swapaxes(0, 1)
        if other is None:
            return mine
        other, _ = lax.optimization_barrier((other, after))
        return mine + other
    block = pl.BlockSpec((groups, 1, rank, rows), lambda pair, side_ref: (0, pair, 0, 0))
    in_specs = [
        pl.BlockSpec((count, groups * rows), lambda pair, side_ref: (0, 2 * pair + side_ref[0])),
        pl.BlockSpec((count, rank), lambda pair, side_ref: (0, 0)),
        pl.BlockSpec((1, count), lambda pair, side_ref: (0, 0)),
    ]
    operands = [inputs, cotangent, tokens[None, :]]
    if other is not None:
        in_specs += [block, pl.BlockSpec(memory_space=pl.ANY)]
        operands += [other, after]
    return pl.pallas_call(
        gradient_kernel,
        grid_spec=pltpu.PrefetchScalarGridSpec(
            num_scalar_prefetch=1,
            grid=(pairs,),
            in_specs=in_specs,
            out_specs=block,
            scratch_shapes=[pltpu.VMEM((rank, count), jnp.bfloat16)],
        ),
        out_shape=jax.ShapeDtypeStruct((groups, pairs, rank, rows), jnp.float32),
        compiler_params=pltpu.CompilerParams(vmem_limit_bytes=8 << 20),
        cost_estimate=pl.CostEstimate(
            flops=count * width * rank, bytes_accessed=count * width + 4 * width * rank, transcendentals=0
        ),
        name="half_gradient",
    )(side[None], *operands)


def signs_kernel(rows, groups, rank, first, seed_ref, *refs):
    block = first + pl.program_id(0)
    tiles = seed_ref.shape[0] * FEAT_BLOCK // TILE_FEATS
    start = step_start(rows, rank, groups, block // tiles)
    base = hash_base(seed_ref, block % tiles, start, strides(rows, rank)[1])
    write_signs(base, rows, rank, 0, KEPT_ROWS, refs[-1])


def kept_signs(seeds, rows, groups, rank, first, count, after, alias):
    features = seeds.shape[0] * FEAT_BLOCK
    steps, tiles = rows * rank // STEP_ROWS, features // TILE_FEATS
    size = count * KEPT_ROWS * TILE_FEATS
    return pl.pallas_call(
        functools.partial(signs_kernel, rows, groups, rank, first),
        grid=(count,),
        in_specs=[pl.BlockSpec(memory_space=pltpu.SMEM)]
        + [pl.BlockSpec(memory_space=pl.ANY)],
        out_specs=pl.BlockSpec(
            (KEPT_ROWS, TILE_FEATS), lambda index: ((index + first) // tiles, (index + first) % tiles)
        ),
        out_shape=jax.ShapeDtypeStruct((steps * KEPT_ROWS, features), FP8),
        input_output_aliases={1: 0} if alias else {},
        compiler_params=pltpu.CompilerParams(vmem_limit_bytes=16 << 20),
        cost_estimate=pl.CostEstimate(flops=size * 10, bytes_accessed=size, transcendentals=0),
        name="kept_signs",
    )(seeds, after)


def direction_kernel(rows, gradient_ref, first_ref, second_ref, out_ref, scale_ref, held, first, second):
    sequences, major, minor = gradient_ref.shape
    mine = pl.ds(pl.multiple_of(lax.axis_index("groups") * rows, 8), rows)
    turn = major != rows
    first[...] = first_ref[mine, :].T if turn else first_ref[mine, :]
    second[...] = second_ref[mine, :].T if turn else second_ref[mine, :]

    def moments(block, largest):
        at = pl.ds(pl.multiple_of(block * 8, 8), 8)
        gradient = gradient_ref[:, at, :]
        moment_one = beta_one * first[at, :][None] + (1 - beta_one) * gradient
        moment_two = beta_two * second[at, :][None] + (1 - beta_two) * gradient * gradient
        direction = moment_one / (jnp.sqrt(moment_two) + epsilon)
        direction = direction.astype(jnp.bfloat16).astype(jnp.float32)
        direction = jnp.swapaxes(direction, 0, 1)
        for row in range(8):
            held[block * 8 + row] = direction[row]
        return jnp.maximum(largest, jnp.max(jnp.abs(direction), axis=0))

    largest = lax.fori_loop(0, major // 8, moments, jnp.zeros((sequences, minor), jnp.float32))
    largest = jnp.broadcast_to(jnp.max(largest, axis=1, keepdims=True), (sequences, minor))
    scale = jnp.ones_like(largest)
    for power in (64, 32, 16, 8, 4, 2, 1):
        room = largest * (2.0**power) < RADIX
        largest = jnp.where(room, largest * (2.0**power), largest)
        scale = jnp.where(room, scale * (2.0**power), scale)
    for power in (2, 1):
        over = largest >= RADIX
        largest = jnp.where(over, largest * (0.5**power), largest)
        scale = jnp.where(over, scale * (0.5**power), scale)
    scale_ref[...] = scale

    def split(row, _):
        rest = held[row] * scale
        digits = []
        for _ in range(DIGITS):
            digit = jnp.round(rest)
            digits.append(digit)
            rest = (rest - digit) * RADIX
        out_ref[:, pl.ds(pl.multiple_of(row * minor, minor), minor)] = jnp.concatenate(digits, axis=0).astype(FP8)
        return 0

    lax.fori_loop(0, major, split, 0, unroll=8)


def scaled_direction(gradient, first, second, rows):
    sequences, major, minor = gradient.shape
    return pl.pallas_call(
        functools.partial(direction_kernel, rows),
        out_shape=(
            jax.ShapeDtypeStruct((DIGITS * sequences, major * minor), FP8),
            jax.ShapeDtypeStruct((sequences, minor), jnp.float32),
        ),
        scratch_shapes=[
            pltpu.VMEM((major, sequences, minor), jnp.float32),
            pltpu.VMEM((major, minor), jnp.float32),
            pltpu.VMEM((major, minor), jnp.float32),
        ],
        compiler_params=pltpu.CompilerParams(vmem_limit_bytes=24 << 20),
        cost_estimate=pl.CostEstimate(
            flops=20 * gradient.size, bytes_accessed=5 * gradient.size, transcendentals=2 * gradient.size
        ),
        name="direction",
    )(gradient, first, second)


def project_kernel(rows, groups, rank, final_scale, seed_ref, direction_ref, scale_ref, kept_ref, out_ref, total, *tiles):
    tile, step = pl.program_id(0), pl.program_id(1)
    sequences = scale_ref.shape[0]
    start = step_start(rows, rank, groups, step)
    last_rows = TILES[-1]

    def multiply(at, signs):
        at = pl.ds(pl.multiple_of(at, 256), signs.shape[0])
        total[...] += jnp.dot(direction_ref[:, at], signs[...], preferred_element_type=jnp.float32)

    @pl.when(step == 0)
    def _():
        total[...] = jnp.zeros_like(total)
        tiles[-1][...] = jnp.zeros_like(tiles[-1])

    here = step * STEP_ROWS
    offset = KEPT_ROWS
    base = hash_base(seed_ref, tile, start, strides(rows, rank)[1])
    for index, count in enumerate(TILES):
        write_signs(base, rows, rank, offset, count, tiles[index])
        if index == 0:
            multiply(jnp.maximum(here - last_rows, 0), tiles[-1])
            multiply(here, kept_ref)
        else:
            multiply(here + offset - TILES[index - 1], tiles[index - 1])
        offset += count

    @pl.when(step == pl.num_programs(1) - 1)
    def _():
        multiply(here + STEP_ROWS - last_rows, tiles[-1])
        inverse = (1.0 / scale_ref[...])[:, :1]
        value = total[(DIGITS - 1) * sequences :, :]
        for digit in reversed(range(DIGITS - 1)):
            value = total[digit * sequences : (digit + 1) * sequences, :] + value * (1.0 / RADIX)
        value = value * inverse * final_scale
        for sequence in range(sequences):
            out_ref[0, sequence] = value[sequence : sequence + 1, :]


def project(seeds, direction, scale, kept, rows, groups, rank, final_scale):
    features = seeds.shape[0] * FEAT_BLOCK
    sequences = scale.shape[0]
    params = rows * rank
    steps = params // STEP_ROWS
    return pl.pallas_call(
        functools.partial(project_kernel, rows, groups, rank, final_scale),
        grid=(features // TILE_FEATS, steps),
        in_specs=[
            pl.BlockSpec(memory_space=pltpu.SMEM),
            pl.BlockSpec((DIGITS * sequences, params), lambda tile, step: (0, 0)),
            pl.BlockSpec(scale.shape, lambda tile, step: (0, 0)),
            pl.BlockSpec((KEPT_ROWS, TILE_FEATS), lambda tile, step: (step, tile)),
        ],
        out_specs=pl.BlockSpec((1, sequences, 1, TILE_FEATS), lambda tile, step: (tile, 0, 0, 0)),
        out_shape=jax.ShapeDtypeStruct((features // TILE_FEATS, sequences, 1, TILE_FEATS), jnp.float32),
        scratch_shapes=[pltpu.VMEM((DIGITS * sequences, TILE_FEATS), jnp.float32)]
        + [pltpu.VMEM((count, TILE_FEATS), FP8) for count in TILES],
        compiler_params=pltpu.CompilerParams(vmem_limit_bytes=32 << 20),
        cost_estimate=pl.CostEstimate(
            flops=10 * params * features, bytes_accessed=params * features // 4, transcendentals=0
        ),
        name="project",
    )(seeds, direction, scale, kept)


def local(
    hidden_input_rows,
    rank_cotangent,
    token_identifiers,
    adam_first_moment,
    adam_second_moment,
    block_seeds,
):
    groups, device_list = lax.axis_size("groups"), lax.axis_size("dp")
    hidden_width = hidden_input_rows.shape[1]
    rank = rank_cotangent.shape[1]
    rows = adam_first_moment.shape[0] // groups
    half = device_list // 2
    core = lax.axis_index("dp") & 1
    blocks = rows * rank // STEP_ROWS * (block_seeds.shape[0] * FEAT_BLOCK // TILE_FEATS)
    early = min(EARLY_BLOCKS, blocks // 2)
    held = (rank_cotangent, token_identifiers)

    given = half_gradient(hidden_input_rows, *held, 1 - core, groups, rows)
    pairs = [(source, source ^ 1) for source in range(device_list)]
    other = lax.ppermute(given, "dp", pairs)
    kept = kept_signs(block_seeds, rows, groups, rank, 0, early, given, False)
    summed = half_gradient(hidden_input_rows, *held, core, groups, rows, other, kept)
    everyone = [
        [group * device_list + 2 * pair + side for group in range(groups) for pair in range(half)]
        for side in range(2)
    ]
    summed = summed.reshape((groups * half,) + summed.shape[2:])
    gradient = lax.all_to_all(
        summed, ("groups", "dp"), split_axis=0, concat_axis=0, axis_index_groups=everyone, tiled=True
    )
    kept = kept_signs(block_seeds, rows, groups, rank, early, blocks - early, kept, True)
    direction, scale = scaled_direction(gradient, adam_first_moment, adam_second_moment, rows)
    final_scale = 1.0 / math.sqrt(hidden_width * rank)
    partial = project(block_seeds, direction, scale, kept, rows, groups, rank, final_scale)
    partial = partial.reshape((groups * device_list, 1, TILE_FEATS))
    by_half = [
        group * device_list + 2 * pair + side for side in range(2) for group in range(groups) for pair in range(half)
    ]
    partial = lax.all_to_all(
        partial, ("groups", "dp"), split_axis=0, concat_axis=0, axis_index_groups=[by_half], tiled=True
    )
    return jnp.sum(partial, axis=0)


def solution(mesh):
    in_specs = (
        P(("groups", "dp"), None),
        P(("groups", "dp"), None),
        P(("groups", "dp")),
        P("dp", None),
        P("dp", None),
        P(),
    )
    out_specs = P(("groups", "dp"), None)
    return jax.shard_map(local, mesh=mesh, in_specs=in_specs, out_specs=out_specs, check_vma=False)
```

time: 225 us -> 198 us (0.88)
  Pallas kernels: 181 us -> 164 us
  waiting for transfers between devices: 12.3 us -> 5.35 us
  other arithmetic: 3.01 us -> 0.76 us
    pallas_call x1, Pallas kernels: 117 us -> 105 us  [project(): pl.pallas_call(functools.partial(project_kernel, rows, groups, rank, fina...]
    pallas_call x3 -> x4, Pallas kernels: 61.5 us -> 56.3 us  [the longest x2 50 us: kept_signs(): pl.pallas_call(functools.partial(signs_kernel, rows, groups, rank, first)...]
    ppermute x1, waiting for transfers between devices: 4 us -> 0.01 us  [local(): other = lax.ppermute(given, 'dp', pairs)]
    all_to_all x1, waiting for transfers between devices: 8.33 us -> 5.35 us  [local(): lax.all_to_all(summed, ('groups', 'dp'), split_axis=0, concat_axis=0, axi...]
  transfers between devices with their start and end apart: 2 -> 2, of which waited for: 2 -> 1; matrix products, arithmetic and copies ran while one was open for 0% -> 0% of each run, Pallas kernels for 17% -> 25%
where the time goes in v2:
time: 198 us
  Pallas kernels  164 us (83%)
  blocking collectives  14.9 us (8%)
  starting transfers between devices  8.49 us (4%)
  waiting for transfers between devices  5.35 us (3%)
  local copies, waits for them, and re-layouts  3.74 us (2%)
    pallas_call x1, Pallas kernels, project(): pl.pallas_call(functools.partial(project_kernel, rows, groups, rank, fina...  105 us
    pallas_call x2, Pallas kernels, kept_signs(): pl.pallas_call(functools.partial(signs_kernel, rows, groups, rank, first)...  50 us
    all_to_all x1, blocking collectives, local(): lax.all_to_all(partial, ('groups', 'dp'), split_axis=0, concat_axis=0, ax...  14.9 us
    all_to_all x1, starting transfers between devices, local(): lax.all_to_all(summed, ('groups', 'dp'), split_axis=0, concat_axis=0, axi...  7.93 us
    pallas_call x2, Pallas kernels, half_gradient(): pl.pallas_call(gradient_kernel, grid_spec=pltpu.PrefetchScalarGridSpec(nu...  6.26 us
    all_to_all x1, waiting for transfers between devices, local(): lax.all_to_all(summed, ('groups', 'dp'), split_axis=0, concat_axis=0, axi...  5.35 us
  transfers between devices with their start and end apart: 2, of which 1 were waited for; matrix products, arithmetic and copies ran while one was open for 0% of the time, Pallas kernels for 25%

profile of v2, /device:TPU:0, one launch (start us, length us, event | category | flops | bytes accessed | tf_op | source)
XLA Modules:
  0.0 197.7 jit_solution(11177231726515692442)
XLA Ops:
  0.0 0.0 copy-start
  0.0 2.2 %copy-done = bf16[256,8192]{1,0:T(8,128)(2,1)S(1)} copy-done((bf16[256,8192]{1,0:T(8,128)(2,1)S(1)}, bf16[256,8192]{1,0:T(8,128)(2,1)}, u32[]{:S(2)}) %copy-start) | copy-done | bytes 4194328
  2.2 0.0 copy-start.2
  2.2 0.8 copy-done.2
  3.0 0.0 copy-start.7
  3.0 0.7 copy-done.7
  3.7 0.0 copy-start.6
  3.7 2.0 %half_gradient.2.refs_0_ = f32[2,8,128,256]{3,2,1,0:T(8,128)S(1)} custom-call(s32[1]{0:T(128)} %bitcast.2.side_ref, bf16[256,8192]{1,0:T(8,128)(2,1)S(1)} %copy-done, bf16[256,128]{1,0:T(8,128)(2,1)S(1)} %copy-done.2, s32[1,256]{1,0:T(1,128)S(1)} %bitcast.7), custom_call_target="tpu_custom_call" | custom-call | flops 268435456 | bytes 6291456 | tf_op jit(solution)/shard_map/half_gradient/pallas_call | solution.py:118
  5.8 0.0 copy-start.3
  5.8 0.0 copy-start.8
  5.8 0.6 collective-permute-start
  6.3 0.0 copy-done.6
  6.3 0.0 copy-start.1
  6.3 7.8 %kept_signs.2.refs_1_.refs_0_ = f8e4m3fn[10240,4096]{1,0:T(32,128)(4,1)} custom-call(s32[8]{0:T(128)S(1)} %copy-done.6, f32[2,8,128,256]{3,2,1,0:T(8,128)S(1)} %half_gradient.2.refs_0_), custom_call_target="tpu_custom_call" | custom-call | flops 52428800 | bytes 5242880 | tf_op jit(solution)/shard_map/kept_signs/pallas_call | solution.py:148
  14.1 0.0 collective-permute-done.refs_0_
  14.1 0.0 copy-done.3
  14.1 0.0 copy-done.8
  14.1 0.0 copy-done.1
  14.2 4.2 %half_gradient.3 = f32[2,8,128,256]{3,2,1,0:T(8,128)} custom-call(s32[1]{0:T(128)} %bitcast.side_ref, bf16[256,8192]{1,0:T(8,128)(2,1)S(1)} %copy-done.1, bf16[256,128]{1,0:T(8,128)(2,1)S(1)} %copy-done.3, s32[1,256]{1,0:T(1,128)S(1)} %bitcast.8, f32[2,8,128,256]{3,2,1,0:T(8,128)S(1)} %collective-permute-done.refs_0_, ...), custom_call_target="tpu_custom_call" | custom-call | flops 268435456 | bytes 6291456 | tf_op jit(solution)/shard_map/half_gradient/pallas_call | solution.py:118
  18.4 7.9 %all-to-all-start = ((f32[16,128,256]{2,1,0:T(8,128)}), f32[16,128,256]{2,1,0:T(8,128)S(1)}, u32[]{:S(2)}, u32[]{:S(2)}) async-start(f32[16,128,256]{2,1,0:T(8,128)} %bitcast.3), calls=%async_computation | async-start | bytes 4194304 | tf_op jit(solution)/shard_map/all_to_all | solution.py:323
  26.3 0.0 copy-start.4
  26.3 0.0 copy-start.5
  26.3 42.2 %kept_signs.3.kept_ref = f8e4m3fn[10240,4096]{1,0:T(32,128)(4,1)} custom-call(s32[8]{0:T(128)S(1)} %copy-done.6, f8e4m3fn[10240,4096]{1,0:T(32,128)(4,1)} %kept_signs.2.refs_1_.refs_0_), custom_call_target="tpu_custom_call", output_to_operand_aliasing={{}: (1, {})} | custom-call | flops 367001600 | bytes 36700160 | tf_op jit(solution)/shard_map/kept_signs/pallas_call | solution.py:148
  68.6 5.3 %all-to-all-done.gradient_ref = f32[16,128,256]{2,1,0:T(8,128)S(1)} async-done(((f32[16,128,256]{2,1,0:T(8,128)}), f32[16,128,256]{2,1,0:T(8,128)S(1)}, u32[]{:S(2)}, u32[]{:S(2)}) %all-to-all-start) | async-done | bytes 2097184 | tf_op jit(solution)/shard_map/all_to_all | solution.py:323
  73.9 0.0 copy-done.4
  73.9 0.0 copy-done.5
  73.9 3.1 %direction.1 = (f8e4m3fn[64,32768]{1,0:T(32,128)(4,1)S(1)}, f32[16,256]{1,0:T(8,128)S(1)}) custom-call(f32[16,128,256]{2,1,0:T(8,128)S(1)} %all-to-all-done.gradient_ref, f32[512,128]{1,0:T(8,128)S(1)} %copy-done.4, f32[512,128]{1,0:T(8,128)S(1)} %copy-done.5), custom_call_target="tpu_custom_call" | custom-call | flops 10485760 | bytes 2621440 | tf_op jit(solution)/shard_map/direction/pallas_call | solution.py:211
  77.0 105.0 %project.1 = f32[2,16,1,2048]{3,2,1,0:T(1,128)S(1)} custom-call(s32[8]{0:T(128)S(1)} %copy-done.6, f8e4m3fn[64,32768]{1,0:T(32,128)(4,1)S(1)} %get-tuple-element.7.direction_ref, f32[16,256]{1,0:T(8,128)S(1)} %get-tuple-element.8.scale_ref, f8e4m3fn[10240,4096]{1,0:T(32,128)(4,1)} %kept_signs.3.kept_ref), custom_call_target="tpu_custom_call" | custom-call | flops 1342177280 | bytes 33554432 | tf_op jit(solution)/shard_map/project/pallas_call | solution.py:274
  182.0 14.9 %all_to_all.10 = f32[32,1,2048]{2,1,0:T(1,128)S(1)} all-to-all(f32[32,1,2048]{2,1,0:T(1,128)S(1)} %bitcast.6), channel_id=1, replica_groups={{0,2,4,6,8,10,12,14,16,18,20,22,24,26,28,30,1,3,5,7,9,11,13,15,17,19,21..., dimensions={0} | all-to-all | bytes 524288 | tf_op jit(solution)/shard_map/all_to_all | solution.py:334
  196.9 0.8 reduce_sum.11
Async XLA Ops:
  0.0 2.2 %copy-start = (bf16[256,8192]{1,0:T(8,128)(2,1)S(1)}, bf16[256,8192]{1,0:T(8,128)(2,1)}, u32[]{:S(2)}) copy-start(bf16[256,8192]{1,0:T(8,128)(2,1)} %inputs_ref.3) | copy-start | bytes 12582916
  2.2 0.8 copy-start.2
  3.0 0.7 copy-start.7
  3.7 2.6 %copy-start.6 = (s32[8]{0:T(128)S(1)}, s32[8]{0:T(128)}, u32[]{:S(2)}) copy-start(s32[8]{0:T(128)} %seed_ref.5) | copy-start | bytes 100
  5.8 8.4 %copy-start.3 = (bf16[256,128]{1,0:T(8,128)(2,1)S(1)}, bf16[256,128]{1,0:T(8,128)(2,1)}, u32[]{:S(2)}) copy-start(bf16[256,128]{1,0:T(8,128)(2,1)} %cotangent_ref.3) | copy-start | bytes 196612
  5.8 8.4 %copy-start.8 = (s32[256]{0:T(256)S(1)}, s32[256]{0:T(256)}, u32[]{:S(2)}) copy-start(s32[256]{0:T(256)} %param.8) | copy-start | bytes 3076
  5.8 8.4 %collective-permute-start = (f32[2,8,128,256]{3,2,1,0:T(8,128)S(1)}, f32[2,8,128,256]{3,2,1,0:T(8,128)S(1)}, u32[]{:S(2)}, u32[]{:S(2)}) collective-permute-start(f32[2,8,128,256]{3,2,1,0:T(8,128)S(1)} %half_gradient.2.refs_0_), channel_id=1, source_target_pairs={{0,1},{1,0},{2,3},{3,2},{4,5},{5,4},{6,7},{7,6},{8,9},{9,8},{10,11... | collective-permute-start | bytes 6291464 | tf_op jit(solution)/shard_map/ppermute | solution.py:315
  6.3 7.8 %copy-start.1 = (bf16[256,8192]{1,0:T(8,128)(2,1)S(1)}, bf16[256,8192]{1,0:T(8,128)(2,1)}, u32[]{:S(2)}) copy-start(bf16[256,8192]{1,0:T(8,128)(2,1)} %inputs_ref.3) | copy-start | bytes 12582916
  18.4 55.5 %all-to-all-start = ((f32[16,128,256]{2,1,0:T(8,128)}), f32[16,128,256]{2,1,0:T(8,128)S(1)}, u32[]{:S(2)}, u32[]{:S(2)}) async-start(f32[16,128,256]{2,1,0:T(8,128)} %bitcast.3), calls=%async_computation | async-start | bytes 4194304 | tf_op jit(solution)/shard_map/all_to_all | solution.py:323
  26.3 47.6 %copy-start.4 = (f32[512,128]{1,0:T(8,128)S(1)}, f32[512,128]{1,0:T(8,128)}, u32[]{:S(2)}) copy-start(f32[512,128]{1,0:T(8,128)} %first_ref.1) | copy-start | bytes 786436
  26.3 47.6 %copy-start.5 = (f32[512,128]{1,0:T(8,128)S(1)}, f32[512,128]{1,0:T(8,128)}, u32[]{:S(2)}) copy-start(f32[512,128]{1,0:T(8,128)} %second_ref.1) | copy-start | bytes 786436

commit v3 on v2

--- a/solution.py
+++ b/solution.py
@@ -19,9 +19,10 @@
 RADIX = 16.0
 FP8 = jnp.float8_e4m3fn
 STEP_ROWS = 4096
-KEPT_ROWS = 1280
-TILES = (768, 768, 768, 512)
-EARLY_BLOCKS = 2
+KEPT_ROWS = 1536
+KEPT_BLOCK = 512
+TILES = (1024, 1024, 512)
+EARLY_BLOCKS = 4
 TILE_FEATS = 2048
 
 
@@ -72,29 +73,52 @@
         out_ref[pl.ds(top, 32), :] = jnp.where(hashed < 0, FP8(-1), FP8(1))
 
 
-def gradient_kernel(side_ref, inputs_ref, cotangent_ref, tokens_ref, *refs):
-    *other_refs, out_ref, masked = refs
-    other_refs = other_refs[:1]
-
-    @pl.when(pl.program_id(0) == 0)
-    def _():
-        turned = cotangent_ref[...].astype(jnp.float32).T
-        masked[...] = jnp.where(tokens_ref[...] != 0, turned, 0.0).astype(jnp.bfloat16)
-
-    part = jnp.dot(masked[...], inputs_ref[...], preferred_element_type=jnp.float32)
-    groups, rows = out_ref.shape[0], out_ref.shape[3]
-    for group in range(groups):
-        piece = part[:, group * rows : (group + 1) * rows]
-        for other_ref in other_refs:
-            piece = piece + other_ref[group, 0]
-        out_ref[group, 0] = piece
-
-
-def half_gradient(inputs, cotangent, tokens, side, groups, rows, other=None, after=None):
+def gradient_kernel(away, inputs_ref, cotangent_ref, tokens_ref, *refs):
+    *other_refs, out_ref, inputs, cotangent, tokens, result, sems, out_sems = refs
+    groups, pairs, _, rows = out_ref.shape
+    width = groups * rows
+    side = lax.axis_index("dp") & 1
+    side = 1 - side if away else side
+    small = [
+        pltpu.make_async_copy(cotangent_ref, cotangent, sems.at[pairs]),
+        pltpu.make_async_copy(tokens_ref, tokens, sems.at[pairs + 1]),
+    ]
+    large = []
+    for pair in range(pairs):
+        columns = pl.ds(pl.multiple_of((2 * pair + side) * width, 128), width)
+        large.append(pltpu.make_async_copy(inputs_ref.at[:, columns], inputs.at[pair], sems.at[pair]))
+    for copy in small + large:
+        copy.start()
+    for copy in small:
+        copy.wait()
+    turned = cotangent[...].astype(jnp.float32).T
+    masked = jnp.where(tokens[...] != 0, turned, 0.0).astype(jnp.bfloat16)
+    copies = []
+    for pair in range(pairs):
+        large[pair].wait()
+        part = jnp.dot(masked, inputs[pair], preferred_element_type=jnp.float32)
+        for group in range(groups):
+            piece = part[:, group * rows : (group + 1) * rows]
+            if other_refs:
+                piece = piece + other_refs[0][group, pair]
+            result[group, pair] = piece
+            copies.append(
+                pltpu.make_async_copy(
+                    result.at[group, pair], out_ref.at[group, pair], out_sems.at[group, pair]
+                )
+            )
+            copies[-1].start()
+    for copy in copies:
+        copy.wait()
+
+
+def half_gradient(inputs, cotangent, tokens, away, groups, rows, other=None, after=None):
     count, width = inputs.shape
     rank = cotangent.shape[1]
     pairs = width // (2 * groups * rows)
     if rows % 128:
+        side = lax.axis_index("dp") & 1
+        side = 1 - side if away else side
         masked = jnp.where((tokens != 0)[:, None], cotangent, jnp.bfloat16(0))
         whole = lax.dot_general(
             inputs, masked, (((0,), (0,)), ((), ())), preferred_element_type=jnp.float32
@@ -105,53 +129,53 @@
             return mine
         other, _ = lax.optimization_barrier((other, after))
         return mine + other
-    block = pl.BlockSpec((groups, 1, rank, rows), lambda pair, side_ref: (0, pair, 0, 0))
-    in_specs = [
-        pl.BlockSpec((count, groups * rows), lambda pair, side_ref: (0, 2 * pair + side_ref[0])),
-        pl.BlockSpec((count, rank), lambda pair, side_ref: (0, 0)),
-        pl.BlockSpec((1, count), lambda pair, side_ref: (0, 0)),
-    ]
+    in_specs = [pl.BlockSpec(memory_space=pltpu.HBM)] * 3
     operands = [inputs, cotangent, tokens[None, :]]
     if other is not None:
-        in_specs += [block, pl.BlockSpec(memory_space=pl.ANY)]
+        in_specs += [pl.BlockSpec(memory_space=pltpu.VMEM), pl.BlockSpec(memory_space=pl.ANY)]
         operands += [other, after]
     return pl.pallas_call(
-        gradient_kernel,
-        grid_spec=pltpu.PrefetchScalarGridSpec(
-            num_scalar_prefetch=1,
-            grid=(pairs,),
-            in_specs=in_specs,
-            out_specs=block,
-            scratch_shapes=[pltpu.VMEM((rank, count), jnp.bfloat16)],
-        ),
+        functools.partial(gradient_kernel, away),
+        in_specs=in_specs,
+        out_specs=pl.BlockSpec(memory_space=pl.ANY),
         out_shape=jax.ShapeDtypeStruct((groups, pairs, rank, rows), jnp.float32),
-        compiler_params=pltpu.CompilerParams(vmem_limit_bytes=8 << 20),
+        scratch_shapes=[
+            pltpu.VMEM((pairs, count, groups * rows), jnp.bfloat16),
+            pltpu.VMEM((count, rank), jnp.bfloat16),
+            pltpu.VMEM((1, count), jnp.int32),
+            pltpu.VMEM((groups, pairs, rank, rows), jnp.float32),
+            pltpu.SemaphoreType.DMA((pairs + 2,)),
+            pltpu.SemaphoreType.DMA((groups, pairs)),
+        ],
+        compiler_params=pltpu.CompilerParams(vmem_limit_bytes=None if other is None else 12 << 20),
         cost_estimate=pl.CostEstimate(
             flops=count * width * rank, bytes_accessed=count * width + 4 * width * rank, transcendentals=0
         ),
         name="half_gradient",
-    )(side[None], *operands)
+    )(*operands)
 
 
 def signs_kernel(rows, groups, rank, first, seed_ref, *refs):
     block = first + pl.program_id(0)
     tiles = seed_ref.shape[0] * FEAT_BLOCK // TILE_FEATS
-    start = step_start(rows, rank, groups, block // tiles)
+    part = block // tiles
+    apart = KEPT_ROWS // KEPT_BLOCK
+    start = step_start(rows, rank, groups, part // apart)
+    start += part % apart * (KEPT_BLOCK // minor_size(rows, rank) * strides(rows, rank)[0])
     base = hash_base(seed_ref, block % tiles, start, strides(rows, rank)[1])
-    write_signs(base, rows, rank, 0, KEPT_ROWS, refs[-1])
+    write_signs(base, rows, rank, 0, KEPT_BLOCK, refs[-1])
 
 
 def kept_signs(seeds, rows, groups, rank, first, count, after, alias):
     features = seeds.shape[0] * FEAT_BLOCK
     steps, tiles = rows * rank // STEP_ROWS, features // TILE_FEATS
-    size = count * KEPT_ROWS * TILE_FEATS
+    size = count * KEPT_BLOCK * TILE_FEATS
     return pl.pallas_call(
         functools.partial(signs_kernel, rows, groups, rank, first),
         grid=(count,),
-        in_specs=[pl.BlockSpec(memory_space=pltpu.SMEM)]
-        + [pl.BlockSpec(memory_space=pl.ANY)],
+        in_specs=[pl.BlockSpec(memory_space=pltpu.SMEM), pl.BlockSpec(memory_space=pl.ANY)],
         out_specs=pl.BlockSpec(
-            (KEPT_ROWS, TILE_FEATS), lambda index: ((index + first) // tiles, (index + first) % tiles)
+            (KEPT_BLOCK, TILE_FEATS), lambda index: ((index + first) // tiles, (index + first) % tiles)
         ),
         out_shape=jax.ShapeDtypeStruct((steps * KEPT_ROWS, features), FP8),
         input_output_aliases={1: 0} if alias else {},
@@ -305,16 +329,16 @@
     rank = rank_cotangent.shape[1]
     rows = adam_first_moment.shape[0] // groups
     half = device_list // 2
-    core = lax.axis_index("dp") & 1
-    blocks = rows * rank // STEP_ROWS * (block_seeds.shape[0] * FEAT_BLOCK // TILE_FEATS)
+    kept_rows = rows * rank // STEP_ROWS * KEPT_ROWS
+    blocks = kept_rows // KEPT_BLOCK * (block_seeds.shape[0] * FEAT_BLOCK // TILE_FEATS)
     early = min(EARLY_BLOCKS, blocks // 2)
     held = (rank_cotangent, token_identifiers)
 
-    given = half_gradient(hidden_input_rows, *held, 1 - core, groups, rows)
+    given = half_gradient(hidden_input_rows, *held, True, groups, rows)
     pairs = [(source, source ^ 1) for source in range(device_list)]
     other = lax.ppermute(given, "dp", pairs)
     kept = kept_signs(block_seeds, rows, groups, rank, 0, early, given, False)
-    summed = half_gradient(hidden_input_rows, *held, core, groups, rows, other, kept)
+    summed = half_gradient(hidden_input_rows, *held, False, groups, rows, other, kept)
     everyone = [
         [group * device_list + 2 * pair + side for group in range(groups) for pair in range(half)]
         for side in range(2)

time: 198 us -> 193 us (0.975)
  waiting for transfers between devices: 5.35 us -> 0.01 us
  local copies, waits for them, and re-layouts: 3.74 us -> 1.62 us
  Pallas kernels: 164 us -> 166 us
    pallas_call x2, Pallas kernels: 50 us -> 60.1 us  [kept_signs(): pl.pallas_call(functools.partial(signs_kernel, rows, groups, rank, first)...]
    pallas_call x1, Pallas kernels: 105 us -> 96 us  [project(): pl.pallas_call(functools.partial(project_kernel, rows, groups, rank, fina...]
    all_to_all x1, waiting for transfers between devices: 5.35 us -> 0.01 us  [local(): lax.all_to_all(summed, ('groups', 'dp'), split_axis=0, concat_axis=0, axi...]
    unnamed x18 -> x14, local copies, waits for them, and re-layouts: 3.74 us -> 1.62 us
  transfers between devices with their start and end apart: 2 -> 2, of which waited for: 1 -> 0; matrix products, arithmetic and copies ran while one was open for 0% -> 0% of each run, Pallas kernels for 25% -> 31%
where the time goes in v3:
time: 193 us
  Pallas kernels  166 us (86%)
  blocking collectives  16.1 us (8%)
  starting transfers between devices  8.43 us (4%)
    pallas_call x1, Pallas kernels, project(): pl.pallas_call(functools.partial(project_kernel, rows, groups, rank, fina...  96 us
    pallas_call x2, Pallas kernels, kept_signs(): pl.pallas_call(functools.partial(signs_kernel, rows, groups, rank, first)...  60.1 us
    all_to_all x1, blocking collectives, local(): lax.all_to_all(partial, ('groups', 'dp'), split_axis=0, concat_axis=0, ax...  16.1 us
    all_to_all x1, starting transfers between devices, local(): lax.all_to_all(summed, ('groups', 'dp'), split_axis=0, concat_axis=0, axi...  7.87 us
    pallas_call x2, Pallas kernels, half_gradient(): pl.pallas_call(functools.partial(gradient_kernel, away), in_specs=in_spec...  6.46 us
  transfers between devices with their start and end apart: 2, of which 0 were waited for; matrix products, arithmetic and copies ran while one was open for 0% of the time, Pallas kernels for 31%

profile of v3, /device:TPU:0, one launch (start us, length us, event | category | flops | bytes accessed | tf_op | source)
XLA Modules:
  0.0 192.6 jit_solution(17075274656994726545)
XLA Ops:
  0.0 0.0 copy-start.5
  0.0 3.5 %half_gradient.2.refs_0_ = f32[2,8,128,256]{3,2,1,0:T(8,128)} custom-call(bf16[256,8192]{1,0:T(8,128)(2,1)} %inputs_ref.3, bf16[256,128]{1,0:T(8,128)(2,1)} %cotangent_ref.3, s32[1,256]{1,0:T(1,128)} %bitcast.5), custom_call_target="tpu_custom_call" | custom-call | flops 268435456 | bytes 6291456 | tf_op jit(solution)/shard_map/half_gradient/pallas_call | solution.py:137
  3.6 0.6 collective-permute-start
  4.1 0.0 copy-done.5
  4.1 0.0 copy-start.1
  4.1 1.6 copy-done.1
  5.7 0.0 copy-start
  5.7 0.0 copy-start.2
  5.7 0.0 copy-start.6
  5.7 6.3 %kept_signs.2.refs_1_.refs_0_ = f8e4m3fn[12288,4096]{1,0:T(32,128)(4,1)} custom-call(s32[8]{0:T(128)S(1)} %copy-done.5, f32[2,8,128,256]{3,2,1,0:T(8,128)S(1)} %copy-done.1), custom_call_target="tpu_custom_call" | custom-call | flops 41943040 | bytes 4194304 | tf_op jit(solution)/shard_map/kept_signs/pallas_call | solution.py:173
  12.0 0.0 collective-permute-done.refs_0_
  12.0 0.0 copy-done
  12.0 0.0 copy-done.2
  12.0 0.0 copy-done.6
  12.0 2.9 %half_gradient.3 = f32[2,8,128,256]{3,2,1,0:T(8,128)} custom-call(bf16[256,8192]{1,0:T(8,128)(2,1)S(1)} %copy-done, bf16[256,128]{1,0:T(8,128)(2,1)S(1)} %copy-done.2, s32[1,256]{1,0:T(1,128)S(1)} %bitcast.6, f32[2,8,128,256]{3,2,1,0:T(8,128)S(1)} %collective-permute-done.refs_0_, f8e4m3fn[12288,4096]{1,0:T(32,128)(4,1)} %kept_signs.2.refs_1_.refs_0_), custom_call_target="tpu_custom_call" | custom-call | flops 268435456 | bytes 6291456 | tf_op jit(solution)/shard_map/half_gradient/pallas_call | solution.py:137
  14.9 7.9 %all-to-all-start = ((f32[16,128,256]{2,1,0:T(8,128)}), f32[16,128,256]{2,1,0:T(8,128)S(1)}, u32[]{:S(2)}, u32[]{:S(2)}) async-start(f32[16,128,256]{2,1,0:T(8,128)} %bitcast.1), calls=%async_computation | async-start | bytes 4194304 | tf_op jit(solution)/shard_map/all_to_all | solution.py:347
  22.8 0.0 copy-start.3
  22.8 0.0 copy-start.4
  22.8 53.8 %kept_signs.3.kept_ref = f8e4m3fn[12288,4096]{1,0:T(32,128)(4,1)} custom-call(s32[8]{0:T(128)S(1)} %copy-done.5, f8e4m3fn[12288,4096]{1,0:T(32,128)(4,1)} %kept_signs.2.refs_1_.refs_0_), custom_call_target="tpu_custom_call", output_to_operand_aliasing={{}: (1, {})} | custom-call | flops 461373440 | bytes 46137344 | tf_op jit(solution)/shard_map/kept_signs/pallas_call | solution.py:173
  76.6 0.0 all-to-all-done.gradient_ref
  76.6 0.0 copy-done.3
  76.7 0.0 copy-done.4
  76.7 3.1 %direction.1 = (f8e4m3fn[64,32768]{1,0:T(32,128)(4,1)S(1)}, f32[16,256]{1,0:T(8,128)S(1)}) custom-call(f32[16,128,256]{2,1,0:T(8,128)S(1)} %all-to-all-done.gradient_ref, f32[512,128]{1,0:T(8,128)S(1)} %copy-done.3, f32[512,128]{1,0:T(8,128)S(1)} %copy-done.4), custom_call_target="tpu_custom_call" | custom-call | flops 10485760 | bytes 2621440 | tf_op jit(solution)/shard_map/direction/pallas_call | solution.py:235
  79.7 96.0 %project.1 = f32[2,16,1,2048]{3,2,1,0:T(1,128)S(1)} custom-call(s32[8]{0:T(128)S(1)} %copy-done.5, f8e4m3fn[64,32768]{1,0:T(32,128)(4,1)S(1)} %get-tuple-element.7.direction_ref, f32[16,256]{1,0:T(8,128)S(1)} %get-tuple-element.8.scale_ref, f8e4m3fn[12288,4096]{1,0:T(32,128)(4,1)} %kept_signs.3.kept_ref), custom_call_target="tpu_custom_call" | custom-call | flops 1342177280 | bytes 33554432 | tf_op jit(solution)/shard_map/project/pallas_call | solution.py:298
  175.7 16.1 %all_to_all.10 = f32[32,1,2048]{2,1,0:T(1,128)S(1)} all-to-all(f32[32,1,2048]{2,1,0:T(1,128)S(1)} %bitcast.4), channel_id=1, replica_groups={{0,2,4,6,8,10,12,14,16,18,20,22,24,26,28,30,1,3,5,7,9,11,13,15,17,19,21..., dimensions={0} | all-to-all | bytes 524288 | tf_op jit(solution)/shard_map/all_to_all | solution.py:358
  191.9 0.8 reduce_sum.11
Async XLA Ops:
  0.0 4.1 %copy-start.5 = (s32[8]{0:T(128)S(1)}, s32[8]{0:T(128)}, u32[]{:S(2)}) copy-start(s32[8]{0:T(128)} %seed_ref.5) | copy-start | bytes 100
  3.6 8.4 %collective-permute-start = (f32[2,8,128,256]{3,2,1,0:T(8,128)}, f32[2,8,128,256]{3,2,1,0:T(8,128)S(1)}, u32[]{:S(2)}, u32[]{:S(2)}) collective-permute-start(f32[2,8,128,256]{3,2,1,0:T(8,128)} %half_gradient.2.refs_0_), channel_id=1, source_target_pairs={{0,1},{1,0},{2,3},{3,2},{4,5},{5,4},{6,7},{7,6},{8,9},{9,8},{10,11... | collective-permute-start | bytes 6291464 | tf_op jit(solution)/shard_map/ppermute | solution.py:339
  4.1 1.6 copy-start.1
  5.7 6.3 %copy-start = (bf16[256,8192]{1,0:T(8,128)(2,1)S(1)}, bf16[256,8192]{1,0:T(8,128)(2,1)}, u32[]{:S(2)}) copy-start(bf16[256,8192]{1,0:T(8,128)(2,1)} %inputs_ref.3) | copy-start | bytes 12582916
  5.7 6.3 %copy-start.2 = (bf16[256,128]{1,0:T(8,128)(2,1)S(1)}, bf16[256,128]{1,0:T(8,128)(2,1)}, u32[]{:S(2)}) copy-start(bf16[256,128]{1,0:T(8,128)(2,1)} %cotangent_ref.3) | copy-start | bytes 196612
  5.7 6.3 %copy-start.6 = (s32[256]{0:T(256)S(1)}, s32[256]{0:T(256)}, u32[]{:S(2)}) copy-start(s32[256]{0:T(256)} %param.8) | copy-start | bytes 3076
  14.9 61.7 %all-to-all-start = ((f32[16,128,256]{2,1,0:T(8,128)}), f32[16,128,256]{2,1,0:T(8,128)S(1)}, u32[]{:S(2)}, u32[]{:S(2)}) async-start(f32[16,128,256]{2,1,0:T(8,128)} %bitcast.1), calls=%async_computation | async-start | bytes 4194304 | tf_op jit(solution)/shard_map/all_to_all | solution.py:347
  22.8 53.8 %copy-start.3 = (f32[512,128]{1,0:T(8,128)S(1)}, f32[512,128]{1,0:T(8,128)}, u32[]{:S(2)}) copy-start(f32[512,128]{1,0:T(8,128)} %first_ref.1) | copy-start | bytes 786436
  22.8 53.8 %copy-start.4 = (f32[512,128]{1,0:T(8,128)S(1)}, f32[512,128]{1,0:T(8,128)}, u32[]{:S(2)}) copy-start(f32[512,128]{1,0:T(8,128)} %second_ref.1) | copy-start | bytes 786436

commit v4 on v3

--- a/solution.py
+++ b/solution.py
@@ -20,9 +20,9 @@
 FP8 = jnp.float8_e4m3fn
 STEP_ROWS = 4096
 KEPT_ROWS = 1536
-KEPT_BLOCK = 512
-TILES = (1024, 1024, 512)
-EARLY_BLOCKS = 4
+KEPT_BLOCK = 768
+TILES = (1280, 1024, 256)
+EARLY_BLOCKS = 3
 TILE_FEATS = 2048
 
 
@@ -74,7 +74,13 @@
 
 
 def gradient_kernel(away, inputs_ref, cotangent_ref, tokens_ref, *refs):
-    *other_refs, out_ref, inputs, cotangent, tokens, result, sems, out_sems = refs
+    *ends, inputs, cotangent, tokens, result, sems, out_sems = refs
+    if away:
+        out_ref, token_ref = ends
+        other_ref = None
+        token_ref[0] = 0
+    else:
+        other_ref, _, out_ref = ends
     groups, pairs, _, rows = out_ref.shape
     width = groups * rows
     side = lax.axis_index("dp") & 1
@@ -99,8 +105,8 @@
         part = jnp.dot(masked, inputs[pair], preferred_element_type=jnp.float32)
         for group in range(groups):
             piece = part[:, group * rows : (group + 1) * rows]
-            if other_refs:
-                piece = piece + other_refs[0][group, pair]
+            if other_ref is not None:
+                piece = piece + other_ref[group, pair]
             result[group, pair] = piece
             copies.append(
                 pltpu.make_async_copy(
@@ -125,20 +131,25 @@
         )
         whole = whole.reshape(pairs, 2, groups, rows, rank)
         mine = lax.dynamic_index_in_dim(whole, side, 1, keepdims=False).swapaxes(0, 1)
-        if other is None:
-            return mine
+        if away:
+            return mine, jnp.zeros((1,), jnp.int32)
         other, _ = lax.optimization_barrier((other, after))
         return mine + other
     in_specs = [pl.BlockSpec(memory_space=pltpu.HBM)] * 3
     operands = [inputs, cotangent, tokens[None, :]]
-    if other is not None:
+    out_specs = pl.BlockSpec(memory_space=pl.ANY)
+    out_shape = jax.ShapeDtypeStruct((groups, pairs, rank, rows), jnp.float32)
+    if away:
+        out_specs = (out_specs, pl.BlockSpec(memory_space=pltpu.SMEM))
+        out_shape = (out_shape, jax.ShapeDtypeStruct((1,), jnp.int32))
+    else:
         in_specs += [pl.BlockSpec(memory_space=pltpu.VMEM), pl.BlockSpec(memory_space=pl.ANY)]
         operands += [other, after]
     return pl.pallas_call(
         functools.partial(gradient_kernel, away),
         in_specs=in_specs,
-        out_specs=pl.BlockSpec(memory_space=pl.ANY),
-        out_shape=jax.ShapeDtypeStruct((groups, pairs, rank, rows), jnp.float32),
+        out_specs=out_specs,
+        out_shape=out_shape,
         scratch_shapes=[
             pltpu.VMEM((pairs, count, groups * rows), jnp.bfloat16),
             pltpu.VMEM((count, rank), jnp.bfloat16),
@@ -147,7 +158,7 @@
             pltpu.SemaphoreType.DMA((pairs + 2,)),
             pltpu.SemaphoreType.DMA((groups, pairs)),
         ],
-        compiler_params=pltpu.CompilerParams(vmem_limit_bytes=None if other is None else 12 << 20),
+        compiler_params=pltpu.CompilerParams(vmem_limit_bytes=None if away else 12 << 20),
         cost_estimate=pl.CostEstimate(
             flops=count * width * rank, bytes_accessed=count * width + 4 * width * rank, transcendentals=0
         ),
@@ -173,7 +184,8 @@
     return pl.pallas_call(
         functools.partial(signs_kernel, rows, groups, rank, first),
         grid=(count,),
-        in_specs=[pl.BlockSpec(memory_space=pltpu.SMEM), pl.BlockSpec(memory_space=pl.ANY)],
+        in_specs=[pl.BlockSpec(memory_space=pltpu.SMEM)]
+        + [pl.BlockSpec(memory_space=pl.ANY if alias else pltpu.SMEM)],
         out_specs=pl.BlockSpec(
             (KEPT_BLOCK, TILE_FEATS), lambda index: ((index + first) // tiles, (index + first) % tiles)
         ),
@@ -197,7 +209,7 @@
         gradient = gradient_ref[:, at, :]
         moment_one = beta_one * first[at, :][None] + (1 - beta_one) * gradient
         moment_two = beta_two * second[at, :][None] + (1 - beta_two) * gradient * gradient
-        direction = moment_one / (jnp.sqrt(moment_two) + epsilon)
+        direction = moment_one / (moment_two * lax.rsqrt(moment_two) + epsilon)
         direction = direction.astype(jnp.bfloat16).astype(jnp.float32)
         direction = jnp.swapaxes(direction, 0, 1)
         for row in range(8):
@@ -334,10 +346,10 @@
     early = min(EARLY_BLOCKS, blocks // 2)
     held = (rank_cotangent, token_identifiers)
 
-    given = half_gradient(hidden_input_rows, *held, True, groups, rows)
+    given, token = half_gradient(hidden_input_rows, *held, True, groups, rows)
     pairs = [(source, source ^ 1) for source in range(device_list)]
     other = lax.ppermute(given, "dp", pairs)
-    kept = kept_signs(block_seeds, rows, groups, rank, 0, early, given, False)
+    kept = kept_signs(block_seeds, rows, groups, rank, 0, early, token, False)
     summed = half_gradient(hidden_input_rows, *held, False, groups, rows, other, kept)
     everyone = [
         [group * device_list + 2 * pair + side for group in range(groups) for pair in range(half)]

time: 193 us -> 192 us (level)
  transfers between devices with their start and end apart: 2 -> 2, of which waited for: 0 -> 0; matrix products, arithmetic and copies ran while one was open for 0% -> 0% of each run, Pallas kernels for 31% -> 32%
where the time goes in v4:
time: 192 us
  Pallas kernels  166 us (86%)
  blocking collectives  16.1 us (8%)
  starting transfers between devices  8.47 us (4%)
    pallas_call x1, Pallas kernels, project(): pl.pallas_call(functools.partial(project_kernel, rows, groups, rank, fina...  96 us
    pallas_call x2, Pallas kernels, kept_signs(): pl.pallas_call(functools.partial(signs_kernel, rows, groups, rank, first)...  60.4 us
    all_to_all x1, blocking collectives, local(): lax.all_to_all(partial, ('groups', 'dp'), split_axis=0, concat_axis=0, ax...  16.1 us
    all_to_all x1, starting transfers between devices, local(): lax.all_to_all(summed, ('groups', 'dp'), split_axis=0, concat_axis=0, axi...  7.91 us
    pallas_call x2, Pallas kernels, half_gradient(): pl.pallas_call(functools.partial(gradient_kernel, away), in_specs=in_spec...  6.97 us
  transfers between devices with their start and end apart: 2, of which 0 were waited for; matrix products, arithmetic and copies ran while one was open for 0% of the time, Pallas kernels for 32%

profile of v4, /device:TPU:0, one launch (start us, length us, event | category | flops | bytes accessed | tf_op | source)
XLA Modules:
  0.0 191.6 jit_solution(6479646985306616196)
XLA Ops:
  0.0 0.0 copy-start.4
  0.0 4.1 %half_gradient.2 = (f32[2,8,128,256]{3,2,1,0:T(8,128)}, s32[1]{0:T(128)}) custom-call(bf16[256,8192]{1,0:T(8,128)(2,1)} %inputs_ref.3, bf16[256,128]{1,0:T(8,128)(2,1)} %cotangent_ref.3, s32[1,256]{1,0:T(1,128)} %bitcast.5), custom_call_target="tpu_custom_call" | custom-call | flops 268435456 | bytes 6291456 | tf_op jit(solution)/shard_map/half_gradient/pallas_call | solution.py:148
  4.1 0.6 collective-permute-start
  4.6 0.0 copy-done.4
  4.6 0.0 copy-start
  4.6 0.0 copy-start.1
  4.6 0.0 copy-start.5
  4.6 7.8 %kept_signs.2.refs_1_.refs_0_ = f8e4m3fn[12288,4096]{1,0:T(32,128)(4,1)} custom-call(s32[8]{0:T(128)S(1)} %copy-done.4, s32[1]{0:T(128)} %get-tuple-element.10.refs_0_), custom_call_target="tpu_custom_call" | custom-call | flops 47185920 | bytes 4718592 | tf_op jit(solution)/shard_map/kept_signs/pallas_call | solution.py:184
  12.5 0.0 collective-permute-done.refs_0_
  12.5 0.0 copy-done
  12.5 0.0 copy-done.1
  12.5 0.0 copy-done.5
  12.5 2.9 %half_gradient.3 = f32[2,8,128,256]{3,2,1,0:T(8,128)} custom-call(bf16[256,8192]{1,0:T(8,128)(2,1)S(1)} %copy-done, bf16[256,128]{1,0:T(8,128)(2,1)S(1)} %copy-done.1, s32[1,256]{1,0:T(1,128)S(1)} %bitcast.6, f32[2,8,128,256]{3,2,1,0:T(8,128)S(1)} %collective-permute-done.refs_0_, f8e4m3fn[12288,4096]{1,0:T(32,128)(4,1)} %kept_signs.2.refs_1_.refs_0_), custom_call_target="tpu_custom_call" | custom-call | flops 268435456 | bytes 6291456 | tf_op jit(solution)/shard_map/half_gradient/pallas_call | solution.py:148
  15.4 7.9 %all-to-all-start = ((f32[16,128,256]{2,1,0:T(8,128)}), f32[16,128,256]{2,1,0:T(8,128)S(1)}, u32[]{:S(2)}, u32[]{:S(2)}) async-start(f32[16,128,256]{2,1,0:T(8,128)} %bitcast.1), calls=%async_computation | async-start | bytes 4194304 | tf_op jit(solution)/shard_map/all_to_all | solution.py:359
  23.3 0.0 copy-start.2
  23.4 0.0 copy-start.3
  23.4 52.5 %kept_signs.3.kept_ref = f8e4m3fn[12288,4096]{1,0:T(32,128)(4,1)} custom-call(s32[8]{0:T(128)S(1)} %copy-done.4, f8e4m3fn[12288,4096]{1,0:T(32,128)(4,1)} %kept_signs.2.refs_1_.refs_0_), custom_call_target="tpu_custom_call", output_to_operand_aliasing={{}: (1, {})} | custom-call | flops 456130560 | bytes 45613056 | tf_op jit(solution)/shard_map/kept_signs/pallas_call | solution.py:184
  75.9 0.0 all-to-all-done.gradient_ref
  75.9 0.0 copy-done.2
  75.9 0.0 copy-done.3
  75.9 2.8 %direction.1 = (f8e4m3fn[64,32768]{1,0:T(32,128)(4,1)S(1)}, f32[16,256]{1,0:T(8,128)S(1)}) custom-call(f32[16,128,256]{2,1,0:T(8,128)S(1)} %all-to-all-done.gradient_ref, f32[512,128]{1,0:T(8,128)S(1)} %copy-done.2, f32[512,128]{1,0:T(8,128)S(1)} %copy-done.3), custom_call_target="tpu_custom_call" | custom-call | flops 10485760 | bytes 2621440 | tf_op jit(solution)/shard_map/direction/pallas_call | solution.py:247
  78.7 96.0 %project.1 = f32[2,16,1,2048]{3,2,1,0:T(1,128)S(1)} custom-call(s32[8]{0:T(128)S(1)} %copy-done.4, f8e4m3fn[64,32768]{1,0:T(32,128)(4,1)S(1)} %get-tuple-element.11.direction_ref, f32[16,256]{1,0:T(8,128)S(1)} %get-tuple-element.12.scale_ref, f8e4m3fn[12288,4096]{1,0:T(32,128)(4,1)} %kept_signs.3.kept_ref), custom_call_target="tpu_custom_call" | custom-call | flops 1342177280 | bytes 33554432 | tf_op jit(solution)/shard_map/project/pallas_call | solution.py:310
  174.7 16.1 %all_to_all.10 = f32[32,1,2048]{2,1,0:T(1,128)S(1)} all-to-all(f32[32,1,2048]{2,1,0:T(1,128)S(1)} %bitcast.4), channel_id=1, replica_groups={{0,2,4,6,8,10,12,14,16,18,20,22,24,26,28,30,1,3,5,7,9,11,13,15,17,19,21..., dimensions={0} | all-to-all | bytes 524288 | tf_op jit(solution)/shard_map/all_to_all | solution.py:370
  190.8 0.8 reduce_sum.11
Async XLA Ops:
  0.0 4.6 %copy-start.4 = (s32[8]{0:T(128)S(1)}, s32[8]{0:T(128)}, u32[]{:S(2)}) copy-start(s32[8]{0:T(128)} %seed_ref.5) | copy-start | bytes 100
  4.1 8.4 %collective-permute-start = (f32[2,8,128,256]{3,2,1,0:T(8,128)}, f32[2,8,128,256]{3,2,1,0:T(8,128)S(1)}, u32[]{:S(2)}, u32[]{:S(2)}) collective-permute-start(f32[2,8,128,256]{3,2,1,0:T(8,128)} %get-tuple-element.9), channel_id=1, source_target_pairs={{0,1},{1,0},{2,3},{3,2},{4,5},{5,4},{6,7},{7,6},{8,9},{9,8},{10,11... | collective-permute-start | bytes 6291464 | tf_op jit(solution)/shard_map/ppermute | solution.py:351
  4.6 7.9 %copy-start = (bf16[256,8192]{1,0:T(8,128)(2,1)S(1)}, bf16[256,8192]{1,0:T(8,128)(2,1)}, u32[]{:S(2)}) copy-start(bf16[256,8192]{1,0:T(8,128)(2,1)} %inputs_ref.3) | copy-start | bytes 12582916
  4.6 7.9 %copy-start.1 = (bf16[256,128]{1,0:T(8,128)(2,1)S(1)}, bf16[256,128]{1,0:T(8,128)(2,1)}, u32[]{:S(2)}) copy-start(bf16[256,128]{1,0:T(8,128)(2,1)} %cotangent_ref.3) | copy-start | bytes 196612
  4.6 7.9 %copy-start.5 = (s32[256]{0:T(256)S(1)}, s32[256]{0:T(256)}, u32[]{:S(2)}) copy-start(s32[256]{0:T(256)} %param.8) | copy-start | bytes 3076
  15.4 60.5 %all-to-all-start = ((f32[16,128,256]{2,1,0:T(8,128)}), f32[16,128,256]{2,1,0:T(8,128)S(1)}, u32[]{:S(2)}, u32[]{:S(2)}) async-start(f32[16,128,256]{2,1,0:T(8,128)} %bitcast.1), calls=%async_computation | async-start | bytes 4194304 | tf_op jit(solution)/shard_map/all_to_all | solution.py:359
  23.3 52.6 %copy-start.2 = (f32[512,128]{1,0:T(8,128)S(1)}, f32[512,128]{1,0:T(8,128)}, u32[]{:S(2)}) copy-start(f32[512,128]{1,0:T(8,128)} %first_ref.1) | copy-start | bytes 786436
  23.4 52.5 %copy-start.3 = (f32[512,128]{1,0:T(8,128)S(1)}, f32[512,128]{1,0:T(8,128)}, u32[]{:S(2)}) copy-start(f32[512,128]{1,0:T(8,128)} %second_ref.1) | copy-start | bytes 786436

commit v5 on v3

--- a/solution.py
+++ b/solution.py
@@ -20,9 +20,9 @@
 FP8 = jnp.float8_e4m3fn
 STEP_ROWS = 4096
 KEPT_ROWS = 1536
-KEPT_BLOCK = 512
-TILES = (1024, 1024, 512)
-EARLY_BLOCKS = 4
+TILES = (1280, 1024, 256)
+EARLY_ROWS, EARLY_BLOCK = 1024, 256
+LATER_BLOCK = 512
 TILE_FEATS = 2048
 
 
@@ -74,7 +74,8 @@
 
 
 def gradient_kernel(away, inputs_ref, cotangent_ref, tokens_ref, *refs):
-    *other_refs, out_ref, inputs, cotangent, tokens, result, sems, out_sems = refs
+    *ends, inputs, cotangent, tokens, result, sems, out_sems = refs
+    other_ref, out_ref = (None, ends[0]) if away else (ends[0], ends[2])
     groups, pairs, _, rows = out_ref.shape
     width = groups * rows
     side = lax.axis_index("dp") & 1
@@ -99,8 +100,8 @@
         part = jnp.dot(masked, inputs[pair], preferred_element_type=jnp.float32)
         for group in range(groups):
             piece = part[:, group * rows : (group + 1) * rows]
-            if other_refs:
-                piece = piece + other_refs[0][group, pair]
+            if other_ref is not None:
+                piece = piece + other_ref[group, pair]
             result[group, pair] = piece
             copies.append(
                 pltpu.make_async_copy(
@@ -125,13 +126,13 @@
         )
         whole = whole.reshape(pairs, 2, groups, rows, rank)
         mine = lax.dynamic_index_in_dim(whole, side, 1, keepdims=False).swapaxes(0, 1)
-        if other is None:
+        if away:
             return mine
         other, _ = lax.optimization_barrier((other, after))
         return mine + other
     in_specs = [pl.BlockSpec(memory_space=pltpu.HBM)] * 3
     operands = [inputs, cotangent, tokens[None, :]]
-    if other is not None:
+    if not away:
         in_specs += [pl.BlockSpec(memory_space=pltpu.VMEM), pl.BlockSpec(memory_space=pl.ANY)]
         operands += [other, after]
     return pl.pallas_call(
@@ -147,7 +148,7 @@
             pltpu.SemaphoreType.DMA((pairs + 2,)),
             pltpu.SemaphoreType.DMA((groups, pairs)),
         ],
-        compiler_params=pltpu.CompilerParams(vmem_limit_bytes=None if other is None else 12 << 20),
+        compiler_params=pltpu.CompilerParams(vmem_limit_bytes=None if away else 12 << 20),
         cost_estimate=pl.CostEstimate(
             flops=count * width * rank, bytes_accessed=count * width + 4 * width * rank, transcendentals=0
         ),
@@ -156,33 +157,34 @@
 
 
 def signs_kernel(rows, groups, rank, first, seed_ref, *refs):
-    block = first + pl.program_id(0)
+    out_ref = refs[-1]
+    count = out_ref.shape[0]
     tiles = seed_ref.shape[0] * FEAT_BLOCK // TILE_FEATS
-    part = block // tiles
-    apart = KEPT_ROWS // KEPT_BLOCK
-    start = step_start(rows, rank, groups, part // apart)
-    start += part % apart * (KEPT_BLOCK // minor_size(rows, rank) * strides(rows, rank)[0])
-    base = hash_base(seed_ref, block % tiles, start, strides(rows, rank)[1])
-    write_signs(base, rows, rank, 0, KEPT_BLOCK, refs[-1])
-
-
-def kept_signs(seeds, rows, groups, rank, first, count, after, alias):
+    row = first + pl.program_id(0) // tiles * count
+    start = step_start(rows, rank, groups, row // KEPT_ROWS)
+    start += row % KEPT_ROWS // minor_size(rows, rank) * strides(rows, rank)[0]
+    base = hash_base(seed_ref, pl.program_id(0) % tiles, start, strides(rows, rank)[1])
+    write_signs(base, rows, rank, 0, count, out_ref)
+
+
+def kept_signs(seeds, rows, groups, rank, first, last, block, before=None):
     features = seeds.shape[0] * FEAT_BLOCK
-    steps, tiles = rows * rank // STEP_ROWS, features // TILE_FEATS
-    size = count * KEPT_BLOCK * TILE_FEATS
+    tiles = features // TILE_FEATS
+    size = (last - first) * features
     return pl.pallas_call(
         functools.partial(signs_kernel, rows, groups, rank, first),
-        grid=(count,),
-        in_specs=[pl.BlockSpec(memory_space=pltpu.SMEM), pl.BlockSpec(memory_space=pl.ANY)],
+        grid=((last - first) // block * tiles,),
+        in_specs=[pl.BlockSpec(memory_space=pltpu.SMEM)]
+        + [pl.BlockSpec(memory_space=pl.ANY)] * (before is not None),
         out_specs=pl.BlockSpec(
-            (KEPT_BLOCK, TILE_FEATS), lambda index: ((index + first) // tiles, (index + first) % tiles)
-        ),
-        out_shape=jax.ShapeDtypeStruct((steps * KEPT_ROWS, features), FP8),
-        input_output_aliases={1: 0} if alias else {},
+            (block, TILE_FEATS), lambda index: (first // block + index // tiles, index % tiles)
+        ),
+        out_shape=jax.ShapeDtypeStruct((rows * rank // STEP_ROWS * KEPT_ROWS, features), FP8),
+        input_output_aliases={} if before is None else {1: 0},
         compiler_params=pltpu.CompilerParams(vmem_limit_bytes=16 << 20),
         cost_estimate=pl.CostEstimate(flops=size * 10, bytes_accessed=size, transcendentals=0),
         name="kept_signs",
-    )(seeds, after)
+    )(seeds, *([] if before is None else [before]))
 
 
 def direction_kernel(rows, gradient_ref, first_ref, second_ref, out_ref, scale_ref, held, first, second):
@@ -197,7 +199,7 @@
         gradient = gradient_ref[:, at, :]
         moment_one = beta_one * first[at, :][None] + (1 - beta_one) * gradient
         moment_two = beta_two * second[at, :][None] + (1 - beta_two) * gradient * gradient
-        direction = moment_one / (jnp.sqrt(moment_two) + epsilon)
+        direction = moment_one / (moment_two * lax.rsqrt(moment_two) + epsilon)
         direction = direction.astype(jnp.bfloat16).astype(jnp.float32)
         direction = jnp.swapaxes(direction, 0, 1)
         for row in range(8):
@@ -330,14 +332,13 @@
     rows = adam_first_moment.shape[0] // groups
     half = device_list // 2
     kept_rows = rows * rank // STEP_ROWS * KEPT_ROWS
-    blocks = kept_rows // KEPT_BLOCK * (block_seeds.shape[0] * FEAT_BLOCK // TILE_FEATS)
-    early = min(EARLY_BLOCKS, blocks // 2)
+    early = min(EARLY_ROWS, kept_rows // 3)
     held = (rank_cotangent, token_identifiers)
 
     given = half_gradient(hidden_input_rows, *held, True, groups, rows)
     pairs = [(source, source ^ 1) for source in range(device_list)]
     other = lax.ppermute(given, "dp", pairs)
-    kept = kept_signs(block_seeds, rows, groups, rank, 0, early, given, False)
+    kept = kept_signs(block_seeds, rows, groups, rank, 0, early, EARLY_BLOCK)
     summed = half_gradient(hidden_input_rows, *held, False, groups, rows, other, kept)
     everyone = [
         [group * device_list + 2 * pair + side for group in range(groups) for pair in range(half)]
@@ -347,7 +348,7 @@
     gradient = lax.all_to_all(
         summed, ("groups", "dp"), split_axis=0, concat_axis=0, axis_index_groups=everyone, tiled=True
     )
-    kept = kept_signs(block_seeds, rows, groups, rank, early, blocks - early, kept, True)
+    kept = kept_signs(block_seeds, rows, groups, rank, early, kept_rows, LATER_BLOCK, kept)
     direction, scale = scaled_direction(gradient, adam_first_moment, adam_second_moment, rows)
     final_scale = 1.0 / math.sqrt(hidden_width * rank)
     partial = project(block_seeds, direction, scale, kept, rows, groups, rank, final_scale)

time: 193 us -> 192 us (level)
  transfers between devices with their start and end apart: 2 -> 2, of which waited for: 0 -> 0; matrix products, arithmetic and copies ran while one was open for 0% -> 0% of each run, Pallas kernels for 31% -> 32%
where the time goes in v5:
time: 192 us
  Pallas kernels  166 us (86%)
  blocking collectives  16.1 us (8%)
  starting transfers between devices  8.5 us (4%)
    pallas_call x1, Pallas kernels, project(): pl.pallas_call(functools.partial(project_kernel, rows, groups, rank, fina...  95.7 us
    pallas_call x2, Pallas kernels, kept_signs(): pl.pallas_call(functools.partial(signs_kernel, rows, groups, rank, first)...  61 us
    all_to_all x1, blocking collectives, local(): lax.all_to_all(partial, ('groups', 'dp'), split_axis=0, concat_axis=0, ax...  16.1 us
    all_to_all x1, starting transfers between devices, local(): lax.all_to_all(summed, ('groups', 'dp'), split_axis=0, concat_axis=0, axi...  7.94 us
    pallas_call x2, Pallas kernels, half_gradient(): pl.pallas_call(functools.partial(gradient_kernel, away), in_specs=in_spec...  6.45 us
  transfers between devices with their start and end apart: 2, of which 0 were waited for; matrix products, arithmetic and copies ran while one was open for 0% of the time, Pallas kernels for 32%

profile of v5, /device:TPU:0, one launch (start us, length us, event | category | flops | bytes accessed | tf_op | source)
XLA Modules:
  0.0 191.5 jit_solution(5010888761714972885)
XLA Ops:
  0.0 0.0 copy-start.4
  0.0 3.5 %half_gradient.2 = f32[2,8,128,256]{3,2,1,0:T(8,128)} custom-call(bf16[256,8192]{1,0:T(8,128)(2,1)} %inputs_ref.3, bf16[256,128]{1,0:T(8,128)(2,1)} %cotangent_ref.3, s32[1,256]{1,0:T(1,128)} %bitcast.5), custom_call_target="tpu_custom_call" | custom-call | flops 268435456 | bytes 6291456 | tf_op jit(solution)/shard_map/half_gradient/pallas_call | solution.py:138
  3.5 0.0 copy-start.1
  3.6 0.0 copy-start.5
  3.6 0.6 collective-permute-start
  4.1 0.0 copy-done.4
  4.1 0.0 copy-start
  4.1 6.8 %kept_signs.2.refs_1_.refs_0_ = f8e4m3fn[12288,4096]{1,0:T(32,128)(4,1)} custom-call(s32[8]{0:T(128)S(1)} %copy-done.4), custom_call_target="tpu_custom_call" | custom-call | flops 41943040 | bytes 4194304 | tf_op jit(solution)/shard_map/kept_signs/pallas_call | solution.py:174
  10.9 0.0 collective-permute-done.refs_0_
  10.9 0.0 copy-done.1
  10.9 0.0 copy-done.5
  10.9 0.0 copy-done
  11.0 2.9 %half_gradient.3 = f32[2,8,128,256]{3,2,1,0:T(8,128)} custom-call(bf16[256,8192]{1,0:T(8,128)(2,1)S(1)} %copy-done, bf16[256,128]{1,0:T(8,128)(2,1)S(1)} %copy-done.1, s32[1,256]{1,0:T(1,128)S(1)} %bitcast.6, f32[2,8,128,256]{3,2,1,0:T(8,128)S(1)} %collective-permute-done.refs_0_, f8e4m3fn[12288,4096]{1,0:T(32,128)(4,1)} %kept_signs.2.refs_1_.refs_0_), custom_call_target="tpu_custom_call" | custom-call | flops 268435456 | bytes 6291456 | tf_op jit(solution)/shard_map/half_gradient/pallas_call | solution.py:138
  13.9 7.9 %all-to-all-start = ((f32[16,128,256]{2,1,0:T(8,128)}), f32[16,128,256]{2,1,0:T(8,128)S(1)}, u32[]{:S(2)}, u32[]{:S(2)}) async-start(f32[16,128,256]{2,1,0:T(8,128)} %bitcast.1), calls=%async_computation | async-start | bytes 4194304 | tf_op jit(solution)/shard_map/all_to_all | solution.py:348
  21.8 0.0 copy-start.2
  21.8 0.0 copy-start.3
  21.8 54.3 %kept_signs.3.kept_ref = f8e4m3fn[12288,4096]{1,0:T(32,128)(4,1)} custom-call(s32[8]{0:T(128)S(1)} %copy-done.4, f8e4m3fn[12288,4096]{1,0:T(32,128)(4,1)} %kept_signs.2.refs_1_.refs_0_), custom_call_target="tpu_custom_call", output_to_operand_aliasing={{}: (1, {})} | custom-call | flops 461373440 | bytes 46137344 | tf_op jit(solution)/shard_map/kept_signs/pallas_call | solution.py:174
  76.1 0.0 all-to-all-done.gradient_ref
  76.1 0.0 copy-done.2
  76.1 0.0 copy-done.3
  76.1 2.8 %direction.1 = (f8e4m3fn[64,32768]{1,0:T(32,128)(4,1)S(1)}, f32[16,256]{1,0:T(8,128)S(1)}) custom-call(f32[16,128,256]{2,1,0:T(8,128)S(1)} %all-to-all-done.gradient_ref, f32[512,128]{1,0:T(8,128)S(1)} %copy-done.2, f32[512,128]{1,0:T(8,128)S(1)} %copy-done.3), custom_call_target="tpu_custom_call" | custom-call | flops 10485760 | bytes 2621440 | tf_op jit(solution)/shard_map/direction/pallas_call | solution.py:237
  78.9 95.7 %project.1 = f32[2,16,1,2048]{3,2,1,0:T(1,128)S(1)} custom-call(s32[8]{0:T(128)S(1)} %copy-done.4, f8e4m3fn[64,32768]{1,0:T(32,128)(4,1)S(1)} %get-tuple-element.7.direction_ref, f32[16,256]{1,0:T(8,128)S(1)} %get-tuple-element.8.scale_ref, f8e4m3fn[12288,4096]{1,0:T(32,128)(4,1)} %kept_signs.3.kept_ref), custom_call_target="tpu_custom_call" | custom-call | flops 1342177280 | bytes 33554432 | tf_op jit(solution)/shard_map/project/pallas_call | solution.py:300
  174.6 16.1 %all_to_all.10 = f32[32,1,2048]{2,1,0:T(1,128)S(1)} all-to-all(f32[32,1,2048]{2,1,0:T(1,128)S(1)} %bitcast.4), channel_id=1, replica_groups={{0,2,4,6,8,10,12,14,16,18,20,22,24,26,28,30,1,3,5,7,9,11,13,15,17,19,21..., dimensions={0} | all-to-all | bytes 524288 | tf_op jit(solution)/shard_map/all_to_all | solution.py:359
  190.8 0.8 reduce_sum.11
Async XLA Ops:
  0.0 4.1 %copy-start.4 = (s32[8]{0:T(128)S(1)}, s32[8]{0:T(128)}, u32[]{:S(2)}) copy-start(s32[8]{0:T(128)} %seed_ref.5) | copy-start | bytes 100
  3.5 7.4 %copy-start.1 = (bf16[256,128]{1,0:T(8,128)(2,1)S(1)}, bf16[256,128]{1,0:T(8,128)(2,1)}, u32[]{:S(2)}) copy-start(bf16[256,128]{1,0:T(8,128)(2,1)} %cotangent_ref.3) | copy-start | bytes 196612
  3.6 7.4 %copy-start.5 = (s32[256]{0:T(256)S(1)}, s32[256]{0:T(256)}, u32[]{:S(2)}) copy-start(s32[256]{0:T(256)} %param.8) | copy-start | bytes 3076
  3.6 7.4 %collective-permute-start = (f32[2,8,128,256]{3,2,1,0:T(8,128)}, f32[2,8,128,256]{3,2,1,0:T(8,128)S(1)}, u32[]{:S(2)}, u32[]{:S(2)}) collective-permute-start(f32[2,8,128,256]{3,2,1,0:T(8,128)} %half_gradient.2), channel_id=1, source_target_pairs={{0,1},{1,0},{2,3},{3,2},{4,5},{5,4},{6,7},{7,6},{8,9},{9,8},{10,11... | collective-permute-start | bytes 6291464 | tf_op jit(solution)/shard_map/ppermute | solution.py:340
  4.1 6.8 %copy-start = (bf16[256,8192]{1,0:T(8,128)(2,1)S(1)}, bf16[256,8192]{1,0:T(8,128)(2,1)}, u32[]{:S(2)}) copy-start(bf16[256,8192]{1,0:T(8,128)(2,1)} %inputs_ref.3) | copy-start | bytes 12582916
  13.9 62.2 %all-to-all-start = ((f32[16,128,256]{2,1,0:T(8,128)}), f32[16,128,256]{2,1,0:T(8,128)S(1)}, u32[]{:S(2)}, u32[]{:S(2)}) async-start(f32[16,128,256]{2,1,0:T(8,128)} %bitcast.1), calls=%async_computation | async-start | bytes 4194304 | tf_op jit(solution)/shard_map/all_to_all | solution.py:348
  21.8 54.3 %copy-start.2 = (f32[512,128]{1,0:T(8,128)S(1)}, f32[512,128]{1,0:T(8,128)}, u32[]{:S(2)}) copy-start(f32[512,128]{1,0:T(8,128)} %first_ref.1) | copy-start | bytes 786436
  21.8 54.3 %copy-start.3 = (f32[512,128]{1,0:T(8,128)S(1)}, f32[512,128]{1,0:T(8,128)}, u32[]{:S(2)}) copy-start(f32[512,128]{1,0:T(8,128)} %second_ref.1) | copy-start | bytes 786436

commit v6 on v5

--- a/solution.py
+++ b/solution.py
@@ -21,8 +21,8 @@
 STEP_ROWS = 4096
 KEPT_ROWS = 1536
 TILES = (1280, 1024, 256)
-EARLY_ROWS, EARLY_BLOCK = 1024, 256
-LATER_BLOCK = 512
+EARLY_ROWS, EARLY_BLOCK = 1536, 512
+LATER_BLOCK = 768
 TILE_FEATS = 2048
 
 
@@ -36,6 +36,11 @@
     hashed = hashed * mix_round
     hashed = hashed ^ lax.shift_right_logical(hashed, jnp.full_like(hashed, 16))
     return hashed * mix_round
+
+
+def feature_tile(turn):
+    core = lax.axis_index("dp") & 1
+    return turn ^ (1 - core)
 
 
 def strides(rows, rank):
@@ -163,7 +168,7 @@
     row = first + pl.program_id(0) // tiles * count
     start = step_start(rows, rank, groups, row // KEPT_ROWS)
     start += row % KEPT_ROWS // minor_size(rows, rank) * strides(rows, rank)[0]
-    base = hash_base(seed_ref, pl.program_id(0) % tiles, start, strides(rows, rank)[1])
+    base = hash_base(seed_ref, feature_tile(pl.program_id(0) % tiles), start, strides(rows, rank)[1])
     write_signs(base, rows, rank, 0, count, out_ref)
 
 
@@ -253,11 +258,16 @@
     )(gradient, first, second)
 
 
-def project_kernel(rows, groups, rank, final_scale, seed_ref, direction_ref, scale_ref, kept_ref, out_ref, total, *tiles):
-    tile, step = pl.program_id(0), pl.program_id(1)
+def project_kernel(turn, rows, groups, rank, final_scale, seed_ref, direction_ref, scale_ref, kept_ref, out_ref, total, kept, sems, *tiles):
+    step, steps = pl.program_id(0), pl.num_programs(0)
     sequences = scale_ref.shape[0]
     start = step_start(rows, rank, groups, step)
     last_rows = TILES[-1]
+    columns = pl.ds(turn * TILE_FEATS, TILE_FEATS)
+
+    def fetch(index):
+        at = pl.ds(pl.multiple_of(index * KEPT_ROWS, KEPT_ROWS), KEPT_ROWS)
+        return pltpu.make_async_copy(kept_ref.at[at, columns], kept.at[index % 2], sems.at[index % 2])
 
     def multiply(at, signs):
         at = pl.ds(pl.multiple_of(at, 256), signs.shape[0])
@@ -265,22 +275,28 @@
 
     @pl.when(step == 0)
     def _():
+        fetch(step).start()
         total[...] = jnp.zeros_like(total)
         tiles[-1][...] = jnp.zeros_like(tiles[-1])
 
+    @pl.when(step + 1 < steps)
+    def _():
+        fetch(step + 1).start()
+
     here = step * STEP_ROWS
     offset = KEPT_ROWS
-    base = hash_base(seed_ref, tile, start, strides(rows, rank)[1])
+    base = hash_base(seed_ref, feature_tile(turn), start, strides(rows, rank)[1])
     for index, count in enumerate(TILES):
         write_signs(base, rows, rank, offset, count, tiles[index])
         if index == 0:
             multiply(jnp.maximum(here - last_rows, 0), tiles[-1])
-            multiply(here, kept_ref)
+            fetch(step).wait()
+            multiply(here, kept.at[step % 2])
         else:
             multiply(here + offset - TILES[index - 1], tiles[index - 1])
         offset += count
 
-    @pl.when(step == pl.num_programs(1) - 1)
+    @pl.when(step == steps - 1)
     def _():
         multiply(here + STEP_ROWS - last_rows, tiles[-1])
         inverse = (1.0 / scale_ref[...])[:, :1]
@@ -289,30 +305,32 @@
             value = total[digit * sequences : (digit + 1) * sequences, :] + value * (1.0 / RADIX)
         value = value * inverse * final_scale
         for sequence in range(sequences):
-            out_ref[0, sequence] = value[sequence : sequence + 1, :]
-
-
-def project(seeds, direction, scale, kept, rows, groups, rank, final_scale):
-    features = seeds.shape[0] * FEAT_BLOCK
+            out_ref[sequence] = value[sequence : sequence + 1, :]
+
+
+def project(turn, seeds, direction, scale, kept, rows, groups, rank, final_scale):
     sequences = scale.shape[0]
     params = rows * rank
-    steps = params // STEP_ROWS
     return pl.pallas_call(
-        functools.partial(project_kernel, rows, groups, rank, final_scale),
-        grid=(features // TILE_FEATS, steps),
+        functools.partial(project_kernel, turn, rows, groups, rank, final_scale),
+        grid=(params // STEP_ROWS,),
         in_specs=[
             pl.BlockSpec(memory_space=pltpu.SMEM),
-            pl.BlockSpec((DIGITS * sequences, params), lambda tile, step: (0, 0)),
-            pl.BlockSpec(scale.shape, lambda tile, step: (0, 0)),
-            pl.BlockSpec((KEPT_ROWS, TILE_FEATS), lambda tile, step: (step, tile)),
+            pl.BlockSpec(memory_space=pltpu.VMEM),
+            pl.BlockSpec(memory_space=pltpu.VMEM),
+            pl.BlockSpec(memory_space=pl.ANY),
         ],
-        out_specs=pl.BlockSpec((1, sequences, 1, TILE_FEATS), lambda tile, step: (tile, 0, 0, 0)),
-        out_shape=jax.ShapeDtypeStruct((features // TILE_FEATS, sequences, 1, TILE_FEATS), jnp.float32),
-        scratch_shapes=[pltpu.VMEM((DIGITS * sequences, TILE_FEATS), jnp.float32)]
+        out_specs=pl.BlockSpec((sequences, 1, TILE_FEATS), lambda step: (0, 0, 0)),
+        out_shape=jax.ShapeDtypeStruct((sequences, 1, TILE_FEATS), jnp.float32),
+        scratch_shapes=[
+            pltpu.VMEM((DIGITS * sequences, TILE_FEATS), jnp.float32),
+            pltpu.VMEM((2, KEPT_ROWS, TILE_FEATS), FP8),
+            pltpu.SemaphoreType.DMA((2,)),
+        ]
         + [pltpu.VMEM((count, TILE_FEATS), FP8) for count in TILES],
         compiler_params=pltpu.CompilerParams(vmem_limit_bytes=32 << 20),
         cost_estimate=pl.CostEstimate(
-            flops=10 * params * features, bytes_accessed=params * features // 4, transcendentals=0
+            flops=10 * params * TILE_FEATS, bytes_accessed=params * TILE_FEATS // 3, transcendentals=0
         ),
         name="project",
     )(seeds, direction, scale, kept)
@@ -351,13 +369,12 @@
     kept = kept_signs(block_seeds, rows, groups, rank, early, kept_rows, LATER_BLOCK, kept)
     direction, scale = scaled_direction(gradient, adam_first_moment, adam_second_moment, rows)
     final_scale = 1.0 / math.sqrt(hidden_width * rank)
-    partial = project(block_seeds, direction, scale, kept, rows, groups, rank, final_scale)
-    partial = partial.reshape((groups * device_list, 1, TILE_FEATS))
-    by_half = [
-        group * device_list + 2 * pair + side for side in range(2) for group in range(groups) for pair in range(half)
-    ]
+    shared = (block_seeds, direction, scale, kept, rows, groups, rank, final_scale)
+    theirs = project(0, *shared)
+    received = lax.ppermute(theirs, "dp", pairs)
+    mine = project(1, *shared)
     partial = lax.all_to_all(
-        partial, ("groups", "dp"), split_axis=0, concat_axis=0, axis_index_groups=[by_half], tiled=True
+        mine + received, ("groups", "dp"), split_axis=0, concat_axis=0, axis_index_groups=everyone, tiled=True
     )
     return jnp.sum(partial, axis=0)
 

time: 192 us -> 198 us (1.031)
  Pallas kernels: 166 us -> 173 us
    pallas_call x1 -> x2, Pallas kernels: 95.7 us -> 104 us  [project(): pl.pallas_call(functools.partial(project_kernel, turn, rows, groups, rank...]
  transfers between devices with their start and end apart: 2 -> 3, of which waited for: 0 -> 0; matrix products, arithmetic and copies ran while one was open for 0% -> 0% of each run, Pallas kernels for 32% -> 57%
where the time goes in v6:
time: 198 us; the launch traced here: 197 us
  Pallas kernels  173 us (87%)
  blocking collectives  14.6 us (7%)
  starting transfers between devices  8.72 us (4%)
    pallas_call x2, Pallas kernels, project(): pl.pallas_call(functools.partial(project_kernel, turn, rows, groups, rank...  104 us
    pallas_call x2, Pallas kernels, kept_signs(): pl.pallas_call(functools.partial(signs_kernel, rows, groups, rank, first)...  60 us
    all_to_all x1, blocking collectives, local(): lax.all_to_all(mine + received, ('groups', 'dp'), split_axis=0, concat_ax...  14.6 us
    all_to_all x1, starting transfers between devices, local(): lax.all_to_all(summed, ('groups', 'dp'), split_axis=0, concat_axis=0, axi...  7.94 us
    pallas_call x2, Pallas kernels, half_gradient(): pl.pallas_call(functools.partial(gradient_kernel, away), in_specs=in_spec...  6.45 us
  transfers between devices with their start and end apart: 3, of which 0 were waited for; matrix products, arithmetic and copies ran while one was open for 0% of the time, Pallas kernels for 57%

profile of v6, /device:TPU:0, one launch (start us, length us, event | category | flops | bytes accessed | tf_op | source)
XLA Modules:
  0.0 197.5 jit_solution(10674501194468320841)
XLA Ops:
  0.0 0.0 copy-start.4
  0.0 3.5 %half_gradient.2 = f32[2,8,128,256]{3,2,1,0:T(8,128)} custom-call(bf16[256,8192]{1,0:T(8,128)(2,1)} %inputs_ref.3, bf16[256,128]{1,0:T(8,128)(2,1)} %cotangent_ref.3, s32[1,256]{1,0:T(1,128)} %bitcast.3), custom_call_target="tpu_custom_call" | custom-call | flops 268435456 | bytes 6291456 | tf_op jit(solution)/shard_map/half_gradient/pallas_call | solution.py:143
  3.5 0.0 copy-start.1
  3.6 0.0 copy-start.5
  3.6 0.6 collective-permute-start
  4.1 0.0 copy-done.4
  4.1 0.0 copy-start
  4.1 8.7 %kept_signs.2.refs_1_.refs_0_ = f8e4m3fn[12288,4096]{1,0:T(32,128)(4,1)} custom-call(s32[8]{0:T(128)S(1)} %copy-done.4), custom_call_target="tpu_custom_call" | custom-call | flops 62914560 | bytes 6291456 | tf_op jit(solution)/shard_map/kept_signs/pallas_call | solution.py:179
  12.8 0.0 collective-permute-done.refs_0_
  12.8 0.0 copy-done.1
  12.8 0.0 copy-done.5
  12.9 0.0 copy-done
  12.9 2.9 %half_gradient.3 = f32[2,8,128,256]{3,2,1,0:T(8,128)} custom-call(bf16[256,8192]{1,0:T(8,128)(2,1)S(1)} %copy-done, bf16[256,128]{1,0:T(8,128)(2,1)S(1)} %copy-done.1, s32[1,256]{1,0:T(1,128)S(1)} %bitcast.4, f32[2,8,128,256]{3,2,1,0:T(8,128)S(1)} %collective-permute-done.refs_0_, f8e4m3fn[12288,4096]{1,0:T(32,128)(4,1)} %kept_signs.2.refs_1_.refs_0_), custom_call_target="tpu_custom_call" | custom-call | flops 268435456 | bytes 6291456 | tf_op jit(solution)/shard_map/half_gradient/pallas_call | solution.py:143
  15.8 7.9 %all-to-all-start = ((f32[16,128,256]{2,1,0:T(8,128)}), f32[16,128,256]{2,1,0:T(8,128)S(1)}, u32[]{:S(2)}, u32[]{:S(2)}) async-start(f32[16,128,256]{2,1,0:T(8,128)} %bitcast.1), calls=%async_computation | async-start | bytes 4194304 | tf_op jit(solution)/shard_map/all_to_all | solution.py:366
  23.7 0.0 copy-start.2
  23.7 0.0 copy-start.3
  23.7 51.3 %kept_signs.3.kept_ref = f8e4m3fn[12288,4096]{1,0:T(32,128)(4,1)} custom-call(s32[8]{0:T(128)S(1)} %copy-done.4, f8e4m3fn[12288,4096]{1,0:T(32,128)(4,1)} %kept_signs.2.refs_1_.refs_0_), custom_call_target="tpu_custom_call", output_to_operand_aliasing={{}: (1, {})} | custom-call | flops 440401920 | bytes 44040192 | tf_op jit(solution)/shard_map/kept_signs/pallas_call | solution.py:179
  75.1 0.0 all-to-all-done.gradient_ref
  75.1 0.0 copy-done.2
  75.1 0.0 copy-done.3
  75.1 2.8 %direction.1 = (f8e4m3fn[64,32768]{1,0:T(32,128)(4,1)S(1)}, f32[16,256]{1,0:T(8,128)S(1)}) custom-call(f32[16,128,256]{2,1,0:T(8,128)S(1)} %all-to-all-done.gradient_ref, f32[512,128]{1,0:T(8,128)S(1)} %copy-done.2, f32[512,128]{1,0:T(8,128)S(1)} %copy-done.3), custom_call_target="tpu_custom_call" | custom-call | flops 10485760 | bytes 2621440 | tf_op jit(solution)/shard_map/direction/pallas_call | solution.py:242
  77.9 51.9 %project.3 = f32[16,1,2048]{2,1,0:T(1,128)S(1)} custom-call(s32[8]{0:T(128)S(1)} %copy-done.4, f8e4m3fn[64,32768]{1,0:T(32,128)(4,1)S(1)} %get-tuple-element.7.direction_ref, f32[16,256]{1,0:T(8,128)S(1)} %get-tuple-element.8.scale_ref, f8e4m3fn[12288,4096]{1,0:T(32,128)(4,1)} %kept_signs.3.kept_ref), custom_call_target="tpu_custom_call" | custom-call | flops 671088640 | bytes 22369620 | tf_op jit(solution)/shard_map/project/pallas_call | solution.py:314
  129.8 0.2 collective-permute-start.1
  130.0 52.0 %project.2 = f32[16,1,2048]{2,1,0:T(1,128)S(1)} custom-call(s32[8]{0:T(128)S(1)} %copy-done.4, f8e4m3fn[64,32768]{1,0:T(32,128)(4,1)S(1)} %get-tuple-element.7.direction_ref, f32[16,256]{1,0:T(8,128)S(1)} %get-tuple-element.8.scale_ref, f8e4m3fn[12288,4096]{1,0:T(32,128)(4,1)} %kept_signs.3.kept_ref), custom_call_target="tpu_custom_call" | custom-call | flops 671088640 | bytes 22369620 | tf_op jit(solution)/shard_map/project/pallas_call | solution.py:314
  182.1 0.0 collective-permute-done.1
  182.1 0.1 add.3
  182.3 14.6 %all_to_all.10 = f32[16,1,2048]{2,1,0:T(1,128)S(1)} all-to-all(f32[16,1,2048]{2,1,0:T(1,128)S(1)} %add.3), channel_id=1, replica_groups={{0,2,4,6,8,10,12,14,16,18,20,22,24,26,28,30},{1,3,5,7,9,11,13,15,17,19,..., dimensions={0} | all-to-all | bytes 262144 | tf_op jit(solution)/shard_map/all_to_all | solution.py:376
  196.8 0.7 reduce_sum.11
Async XLA Ops:
  0.0 4.1 %copy-start.4 = (s32[8]{0:T(128)S(1)}, s32[8]{0:T(128)}, u32[]{:S(2)}) copy-start(s32[8]{0:T(128)} %seed_ref.7) | copy-start | bytes 100
  3.5 9.3 %copy-start.1 = (bf16[256,128]{1,0:T(8,128)(2,1)S(1)}, bf16[256,128]{1,0:T(8,128)(2,1)}, u32[]{:S(2)}) copy-start(bf16[256,128]{1,0:T(8,128)(2,1)} %cotangent_ref.3) | copy-start | bytes 196612
  3.6 9.3 %copy-start.5 = (s32[256]{0:T(256)S(1)}, s32[256]{0:T(256)}, u32[]{:S(2)}) copy-start(s32[256]{0:T(256)} %param.8) | copy-start | bytes 3076
  3.6 9.3 %collective-permute-start = (f32[2,8,128,256]{3,2,1,0:T(8,128)}, f32[2,8,128,256]{3,2,1,0:T(8,128)S(1)}, u32[]{:S(2)}, u32[]{:S(2)}) collective-permute-start(f32[2,8,128,256]{3,2,1,0:T(8,128)} %half_gradient.2), channel_id=1, source_target_pairs={{0,1},{1,0},{2,3},{3,2},{4,5},{5,4},{6,7},{7,6},{8,9},{9,8},{10,11... | collective-permute-start | bytes 6291464 | tf_op jit(solution)/shard_map/ppermute | solution.py:358
  4.1 8.7 %copy-start = (bf16[256,8192]{1,0:T(8,128)(2,1)S(1)}, bf16[256,8192]{1,0:T(8,128)(2,1)}, u32[]{:S(2)}) copy-start(bf16[256,8192]{1,0:T(8,128)(2,1)} %inputs_ref.3) | copy-start | bytes 12582916
  15.8 59.3 %all-to-all-start = ((f32[16,128,256]{2,1,0:T(8,128)}), f32[16,128,256]{2,1,0:T(8,128)S(1)}, u32[]{:S(2)}, u32[]{:S(2)}) async-start(f32[16,128,256]{2,1,0:T(8,128)} %bitcast.1), calls=%async_computation | async-start | bytes 4194304 | tf_op jit(solution)/shard_map/all_to_all | solution.py:366
  23.7 51.4 %copy-start.2 = (f32[512,128]{1,0:T(8,128)S(1)}, f32[512,128]{1,0:T(8,128)}, u32[]{:S(2)}) copy-start(f32[512,128]{1,0:T(8,128)} %first_ref.1) | copy-start | bytes 786436
  23.7 51.4 %copy-start.3 = (f32[512,128]{1,0:T(8,128)S(1)}, f32[512,128]{1,0:T(8,128)}, u32[]{:S(2)}) copy-start(f32[512,128]{1,0:T(8,128)} %second_ref.1) | copy-start | bytes 786436
  129.8 52.3 %collective-permute-start.1 = (f32[16,1,2048]{2,1,0:T(1,128)S(1)}, f32[16,1,2048]{2,1,0:T(1,128)S(1)}, u32[]{:S(2)}, u32[]{:S(2)}) collective-permute-start(f32[16,1,2048]{2,1,0:T(1,128)S(1)} %project.3), channel_id=1, source_target_pairs={{0,1},{1,0},{2,3},{3,2},{4,5},{5,4},{6,7},{7,6},{8,9},{9,8},{10,11... | collective-permute-start | bytes 393224 | tf_op jit(solution)/shard_map/ppermute | solution.py:374

commit v7 on v5

--- a/solution.py
+++ b/solution.py
@@ -21,7 +21,7 @@
 STEP_ROWS = 4096
 KEPT_ROWS = 1536
 TILES = (1280, 1024, 256)
-EARLY_ROWS, EARLY_BLOCK = 1024, 256
+EARLY_ROWS, EARLY_BLOCK = 1024, 512
 LATER_BLOCK = 512
 TILE_FEATS = 2048
 
@@ -73,13 +73,21 @@
         out_ref[pl.ds(top, 32), :] = jnp.where(hashed < 0, FP8(-1), FP8(1))
 
 
-def gradient_kernel(away, inputs_ref, cotangent_ref, tokens_ref, *refs):
-    *ends, inputs, cotangent, tokens, result, sems, out_sems = refs
-    other_ref, out_ref = (None, ends[0]) if away else (ends[0], ends[2])
+def masked_turned(cotangent, tokens):
+    return jnp.where(tokens != 0, cotangent.astype(jnp.float32).T, 0.0).astype(jnp.bfloat16)
+
+
+def put(result, out_ref, sems, group, pair, piece):
+    result[group, pair] = piece
+    copy = pltpu.make_async_copy(result.at[group, pair], out_ref.at[group, pair], sems.at[group, pair])
+    copy.start()
+    return copy
+
+
+def given_kernel(inputs_ref, cotangent_ref, tokens_ref, out_ref, inputs, cotangent, tokens, result, sems, out_sems):
     groups, pairs, _, rows = out_ref.shape
     width = groups * rows
-    side = lax.axis_index("dp") & 1
-    side = 1 - side if away else side
+    side = 1 - (lax.axis_index("dp") & 1)
     small = [
         pltpu.make_async_copy(cotangent_ref, cotangent, sems.at[pairs]),
         pltpu.make_async_copy(tokens_ref, tokens, sems.at[pairs + 1]),
@@ -92,23 +100,29 @@
         copy.start()
     for copy in small:
         copy.wait()
-    turned = cotangent[...].astype(jnp.float32).T
-    masked = jnp.where(tokens[...] != 0, turned, 0.0).astype(jnp.bfloat16)
+    masked = masked_turned(cotangent[...], tokens[...])
     copies = []
     for pair in range(pairs):
         large[pair].wait()
         part = jnp.dot(masked, inputs[pair], preferred_element_type=jnp.float32)
         for group in range(groups):
-            piece = part[:, group * rows : (group + 1) * rows]
-            if other_ref is not None:
-                piece = piece + other_ref[group, pair]
-            result[group, pair] = piece
-            copies.append(
-                pltpu.make_async_copy(
-                    result.at[group, pair], out_ref.at[group, pair], out_sems.at[group, pair]
-                )
-            )
-            copies[-1].start()
+            copies.append(put(result, out_ref, out_sems, group, pair, part[:, group * rows : (group + 1) * rows]))
+    for copy in copies:
+        copy.wait()
+
+
+def summed_kernel(inputs_ref, cotangent_ref, tokens_ref, other_ref, after_ref, out_ref, result, out_sems):
+    groups, pairs, _, rows = out_ref.shape
+    width = groups * rows
+    side = lax.axis_index("dp") & 1
+    masked = masked_turned(cotangent_ref[...], tokens_ref[...])
+    copies = []
+    for pair in range(pairs):
+        columns = pl.ds(pl.multiple_of((2 * pair + side) * width, 128), width)
+        part = jnp.dot(masked, inputs_ref[:, columns], preferred_element_type=jnp.float32)
+        for group in range(groups):
+            piece = part[:, group * rows : (group + 1) * rows] + other_ref[group, pair]
+            copies.append(put(result, out_ref, out_sems, group, pair, piece))
     for copy in copies:
         copy.wait()
 
@@ -130,24 +144,29 @@
             return mine
         other, _ = lax.optimization_barrier((other, after))
         return mine + other
-    in_specs = [pl.BlockSpec(memory_space=pltpu.HBM)] * 3
     operands = [inputs, cotangent, tokens[None, :]]
-    if not away:
-        in_specs += [pl.BlockSpec(memory_space=pltpu.VMEM), pl.BlockSpec(memory_space=pl.ANY)]
+    result = pltpu.VMEM((groups, pairs, rank, rows), jnp.float32)
+    out_sems = pltpu.SemaphoreType.DMA((groups, pairs))
+    if away:
+        in_specs = [pl.BlockSpec(memory_space=pl.ANY)] * 3
+        scratch = [
+            pltpu.VMEM((pairs, count, groups * rows), jnp.bfloat16),
+            pltpu.VMEM((count, rank), jnp.bfloat16),
+            pltpu.VMEM((1, count), jnp.int32),
+            result,
+            pltpu.SemaphoreType.DMA((pairs + 2,)),
+            out_sems,
+        ]
+    else:
+        in_specs = [pl.BlockSpec(memory_space=pltpu.VMEM)] * 4 + [pl.BlockSpec(memory_space=pl.ANY)]
         operands += [other, after]
+        scratch = [result, out_sems]
     return pl.pallas_call(
-        functools.partial(gradient_kernel, away),
+        given_kernel if away else summed_kernel,
         in_specs=in_specs,
         out_specs=pl.BlockSpec(memory_space=pl.ANY),
         out_shape=jax.ShapeDtypeStruct((groups, pairs, rank, rows), jnp.float32),
-        scratch_shapes=[
-            pltpu.VMEM((pairs, count, groups * rows), jnp.bfloat16),
-            pltpu.VMEM((count, rank), jnp.bfloat16),
-            pltpu.VMEM((1, count), jnp.int32),
-            pltpu.VMEM((groups, pairs, rank, rows), jnp.float32),
-            pltpu.SemaphoreType.DMA((pairs + 2,)),
-            pltpu.SemaphoreType.DMA((groups, pairs)),
-        ],
+        scratch_shapes=scratch,
         compiler_params=pltpu.CompilerParams(vmem_limit_bytes=None if away else 12 << 20),
         cost_estimate=pl.CostEstimate(
             flops=count * width * rank, bytes_accessed=count * width + 4 * width * rank, transcendentals=0
@@ -289,7 +308,7 @@
             value = total[digit * sequences : (digit + 1) * sequences, :] + value * (1.0 / RADIX)
         value = value * inverse * final_scale
         for sequence in range(sequences):
-            out_ref[0, sequence] = value[sequence : sequence + 1, :]
+            out_ref[sequence, 0] = value[sequence : sequence + 1, :]
 
 
 def project(seeds, direction, scale, kept, rows, groups, rank, final_scale):
@@ -306,8 +325,8 @@
             pl.BlockSpec(scale.shape, lambda tile, step: (0, 0)),
             pl.BlockSpec((KEPT_ROWS, TILE_FEATS), lambda tile, step: (step, tile)),
         ],
-        out_specs=pl.BlockSpec((1, sequences, 1, TILE_FEATS), lambda tile, step: (tile, 0, 0, 0)),
-        out_shape=jax.ShapeDtypeStruct((features // TILE_FEATS, sequences, 1, TILE_FEATS), jnp.float32),
+        out_specs=pl.BlockSpec((sequences, 1, 1, TILE_FEATS), lambda tile, step: (0, tile, 0, 0)),
+        out_shape=jax.ShapeDtypeStruct((sequences, features // TILE_FEATS, 1, TILE_FEATS), jnp.float32),
         scratch_shapes=[pltpu.VMEM((DIGITS * sequences, TILE_FEATS), jnp.float32)]
         + [pltpu.VMEM((count, TILE_FEATS), FP8) for count in TILES],
         compiler_params=pltpu.CompilerParams(vmem_limit_bytes=32 << 20),
@@ -353,12 +372,7 @@
     final_scale = 1.0 / math.sqrt(hidden_width * rank)
     partial = project(block_seeds, direction, scale, kept, rows, groups, rank, final_scale)
     partial = partial.reshape((groups * device_list, 1, TILE_FEATS))
-    by_half = [
-        group * device_list + 2 * pair + side for side in range(2) for group in range(groups) for pair in range(half)
-    ]
-    partial = lax.all_to_all(
-        partial, ("groups", "dp"), split_axis=0, concat_axis=0, axis_index_groups=[by_half], tiled=True
-    )
+    partial = lax.all_to_all(partial, ("groups", "dp"), split_axis=0, concat_axis=0, tiled=True)
     return jnp.sum(partial, axis=0)
 
 

time: 192 us -> 190 us (0.990)
  Pallas kernels: 166 us -> 164 us
where the time goes in v7:
time: 190 us
  Pallas kernels  164 us (86%)
  blocking collectives  16 us (8%)
  starting transfers between devices  8.5 us (4%)
    pallas_call x1, Pallas kernels, project(): pl.pallas_call(functools.partial(project_kernel, rows, groups, rank, fina...  95.8 us
    pallas_call x2, Pallas kernels, kept_signs(): pl.pallas_call(functools.partial(signs_kernel, rows, groups, rank, first)...  60.5 us
    all_to_all x1, blocking collectives, local(): lax.all_to_all(partial, ('groups', 'dp'), split_axis=0, concat_axis=0, ti...  16 us
    all_to_all x1, starting transfers between devices, local(): lax.all_to_all(summed, ('groups', 'dp'), split_axis=0, concat_axis=0, axi...  7.94 us
    pallas_call x2, Pallas kernels, half_gradient(): pl.pallas_call(given_kernel if away else summed_kernel, in_specs=in_specs...  5.26 us
  transfers between devices with their start and end apart: 2, of which 0 were waited for; matrix products, arithmetic and copies ran while one was open for 0% of the time, Pallas kernels for 32%

profile of v7, /device:TPU:0, one launch (start us, length us, event | category | flops | bytes accessed | tf_op | source)
XLA Modules:
  0.0 189.7 jit_solution(14905186667929862247)
XLA Ops:
  0.0 0.0 copy-start.4
  0.0 3.5 %half_gradient.2 = f32[2,8,128,256]{3,2,1,0:T(8,128)} custom-call(bf16[256,8192]{1,0:T(8,128)(2,1)} %inputs_ref.3, bf16[256,128]{1,0:T(8,128)(2,1)} %cotangent_ref.3, s32[1,256]{1,0:T(1,128)} %bitcast.5), custom_call_target="tpu_custom_call" | custom-call | flops 268435456 | bytes 6291456 | tf_op jit(solution)/shard_map/half_gradient/pallas_call | solution.py:164
  3.5 0.0 copy-start.1
  3.6 0.0 copy-start.5
  3.6 0.6 collective-permute-start
  4.1 0.0 copy-done.4
  4.1 0.0 copy-start
  4.1 6.3 %kept_signs.2.after_ref.refs_0_ = f8e4m3fn[12288,4096]{1,0:T(32,128)(4,1)} custom-call(s32[8]{0:T(128)S(1)} %copy-done.4), custom_call_target="tpu_custom_call" | custom-call | flops 41943040 | bytes 4194304 | tf_op jit(solution)/shard_map/kept_signs/pallas_call | solution.py:193
  10.4 0.0 collective-permute-done.other_ref
  10.4 0.0 copy-done.1
  10.4 0.0 copy-done.5
  10.4 0.0 copy-done
  10.4 1.7 half_gradient.3
  12.1 7.9 %all-to-all-start = ((f32[16,128,256]{2,1,0:T(8,128)}), f32[16,128,256]{2,1,0:T(8,128)S(1)}, u32[]{:S(2)}, u32[]{:S(2)}) async-start(f32[16,128,256]{2,1,0:T(8,128)} %bitcast.1), calls=%async_computation | async-start | bytes 4194304 | tf_op jit(solution)/shard_map/all_to_all | solution.py:367
  20.1 0.0 copy-start.2
  20.1 0.0 copy-start.3
  20.1 54.3 %kept_signs.3.kept_ref = f8e4m3fn[12288,4096]{1,0:T(32,128)(4,1)} custom-call(s32[8]{0:T(128)S(1)} %copy-done.4, f8e4m3fn[12288,4096]{1,0:T(32,128)(4,1)} %kept_signs.2.after_ref.refs_0_), custom_call_target="tpu_custom_call", output_to_operand_aliasing={{}: (1, {})} | custom-call | flops 461373440 | bytes 46137344 | tf_op jit(solution)/shard_map/kept_signs/pallas_call | solution.py:193
  74.4 0.0 all-to-all-done.gradient_ref
  74.4 0.0 copy-done.2
  74.4 0.0 copy-done.3
  74.4 2.8 %direction.1 = (f8e4m3fn[64,32768]{1,0:T(32,128)(4,1)S(1)}, f32[16,256]{1,0:T(8,128)S(1)}) custom-call(f32[16,128,256]{2,1,0:T(8,128)S(1)} %all-to-all-done.gradient_ref, f32[512,128]{1,0:T(8,128)S(1)} %copy-done.2, f32[512,128]{1,0:T(8,128)S(1)} %copy-done.3), custom_call_target="tpu_custom_call" | custom-call | flops 10485760 | bytes 2621440 | tf_op jit(solution)/shard_map/direction/pallas_call | solution.py:256
  77.2 95.8 %project.1 = f32[16,2,1,2048]{3,2,1,0:T(1,128)S(1)} custom-call(s32[8]{0:T(128)S(1)} %copy-done.4, f8e4m3fn[64,32768]{1,0:T(32,128)(4,1)S(1)} %get-tuple-element.7.direction_ref, f32[16,256]{1,0:T(8,128)S(1)} %get-tuple-element.8.scale_ref, f8e4m3fn[12288,4096]{1,0:T(32,128)(4,1)} %kept_signs.3.kept_ref), custom_call_target="tpu_custom_call" | custom-call | flops 1342177280 | bytes 33554432 | tf_op jit(solution)/shard_map/project/pallas_call | solution.py:319
  173.0 16.0 %all_to_all.10 = f32[32,1,2048]{2,1,0:T(1,128)S(1)} all-to-all(f32[32,1,2048]{2,1,0:T(1,128)S(1)} %bitcast.4), channel_id=1, replica_groups=mesh['groups'=2,'dp'=16] {'groups','dp'}, dimensions={0} | all-to-all | bytes 524288 | tf_op jit(solution)/shard_map/all_to_all | solution.py:375
  189.0 0.8 reduce_sum.11
Async XLA Ops:
  0.0 4.1 %copy-start.4 = (s32[8]{0:T(128)S(1)}, s32[8]{0:T(128)}, u32[]{:S(2)}) copy-start(s32[8]{0:T(128)} %seed_ref.5) | copy-start | bytes 100
  3.5 6.8 %copy-start.1 = (bf16[256,128]{1,0:T(8,128)(2,1)S(1)}, bf16[256,128]{1,0:T(8,128)(2,1)}, u32[]{:S(2)}) copy-start(bf16[256,128]{1,0:T(8,128)(2,1)} %cotangent_ref.3) | copy-start | bytes 196612
  3.6 6.8 %copy-start.5 = (s32[256]{0:T(256)S(1)}, s32[256]{0:T(256)}, u32[]{:S(2)}) copy-start(s32[256]{0:T(256)} %param.8) | copy-start | bytes 3076
  3.6 6.8 %collective-permute-start = (f32[2,8,128,256]{3,2,1,0:T(8,128)}, f32[2,8,128,256]{3,2,1,0:T(8,128)S(1)}, u32[]{:S(2)}, u32[]{:S(2)}) collective-permute-start(f32[2,8,128,256]{3,2,1,0:T(8,128)} %half_gradient.2), channel_id=1, source_target_pairs={{0,1},{1,0},{2,3},{3,2},{4,5},{5,4},{6,7},{7,6},{8,9},{9,8},{10,11... | collective-permute-start | bytes 6291464 | tf_op jit(solution)/shard_map/ppermute | solution.py:359
  4.1 6.3 %copy-start = (bf16[256,8192]{1,0:T(8,128)(2,1)S(1)}, bf16[256,8192]{1,0:T(8,128)(2,1)}, u32[]{:S(2)}) copy-start(bf16[256,8192]{1,0:T(8,128)(2,1)} %inputs_ref.3) | copy-start | bytes 12582916
  12.1 62.2 %all-to-all-start = ((f32[16,128,256]{2,1,0:T(8,128)}), f32[16,128,256]{2,1,0:T(8,128)S(1)}, u32[]{:S(2)}, u32[]{:S(2)}) async-start(f32[16,128,256]{2,1,0:T(8,128)} %bitcast.1), calls=%async_computation | async-start | bytes 4194304 | tf_op jit(solution)/shard_map/all_to_all | solution.py:367
  20.1 54.3 %copy-start.2 = (f32[512,128]{1,0:T(8,128)S(1)}, f32[512,128]{1,0:T(8,128)}, u32[]{:S(2)}) copy-start(f32[512,128]{1,0:T(8,128)} %first_ref.1) | copy-start | bytes 786436
  20.1 54.3 %copy-start.3 = (f32[512,128]{1,0:T(8,128)S(1)}, f32[512,128]{1,0:T(8,128)}, u32[]{:S(2)}) copy-start(f32[512,128]{1,0:T(8,128)} %second_ref.1) | copy-start | bytes 786436

commit v8 on v7

--- a/solution.py
+++ b/solution.py
@@ -21,8 +21,9 @@
 STEP_ROWS = 4096
 KEPT_ROWS = 1536
 TILES = (1280, 1024, 256)
-EARLY_ROWS, EARLY_BLOCK = 1024, 512
-LATER_BLOCK = 512
+EARLY_ROWS, EARLY_BLOCK = 768, 384
+LATER_BLOCK = 768
+LANES = 128
 TILE_FEATS = 2048
 
 
@@ -38,17 +39,19 @@
     return hashed * mix_round
 
 
+def turned(rows):
+    return rows % LANES == 0
+
+
 def strides(rows, rank):
-    return (1, rank) if rows % 128 == 0 else (rank, 1)
-
-
-def minor_size(rows, rank):
-    return rows if rows % 128 == 0 else rank
+    return (1, rank) if turned(rows) else (rank, 1)
 
 
 def step_start(rows, rank, groups, step):
     mine = lax.axis_index("dp") * groups + lax.axis_index("groups")
-    return mine * (rows * rank) + step * (STEP_ROWS // minor_size(rows, rank) * strides(rows, rank)[0])
+    line = step * (STEP_ROWS // LANES)
+    apart = line // rank * (LANES * rank) + line % rank if turned(rows) else line * rank
+    return mine * (rows * rank) + apart
 
 
 def hash_base(seed_ref, feature_tile, start, minor_stride):
@@ -63,11 +66,11 @@
 
 
 def write_signs(base, rows, rank, offset, count, out_ref):
-    minor, (major_stride, minor_stride) = minor_size(rows, rank), strides(rows, rank)
+    major_stride, minor_stride = strides(rows, rank)
     for top in range(0, count, 32):
         hashes = []
         for part in range(offset + top, offset + top + 32, 8):
-            apart = part // minor * major_stride + part % minor * minor_stride
+            apart = part // LANES * major_stride + part % LANES * minor_stride
             hashes.append(scramble(base + wrap(mix_param * apart)))
         hashed = jnp.concatenate(hashes, axis=0)
         out_ref[pl.ds(top, 32), :] = jnp.where(hashed < 0, FP8(-1), FP8(1))
@@ -77,16 +80,22 @@
     return jnp.where(tokens != 0, cotangent.astype(jnp.float32).T, 0.0).astype(jnp.bfloat16)
 
 
-def put(result, out_ref, sems, group, pair, piece):
-    result[group, pair] = piece
+def put(result, out_ref, sems, group, pair, part, other_ref=None):
+    rank = part.shape[0]
+    lines = result.shape[2] // rank
+    for line in range(lines):
+        left = (group * lines + line) * LANES
+        at = slice(line * rank, (line + 1) * rank)
+        piece = part[:, left : left + LANES]
+        result[group, pair, at, :] = piece if other_ref is None else piece + other_ref[group, pair, at, :]
     copy = pltpu.make_async_copy(result.at[group, pair], out_ref.at[group, pair], sems.at[group, pair])
     copy.start()
     return copy
 
 
 def given_kernel(inputs_ref, cotangent_ref, tokens_ref, out_ref, inputs, cotangent, tokens, result, sems, out_sems):
-    groups, pairs, _, rows = out_ref.shape
-    width = groups * rows
+    groups, pairs = out_ref.shape[:2]
+    width = inputs.shape[2]
     side = 1 - (lax.axis_index("dp") & 1)
     small = [
         pltpu.make_async_copy(cotangent_ref, cotangent, sems.at[pairs]),
@@ -106,14 +115,14 @@
         large[pair].wait()
         part = jnp.dot(masked, inputs[pair], preferred_element_type=jnp.float32)
         for group in range(groups):
-            copies.append(put(result, out_ref, out_sems, group, pair, part[:, group * rows : (group + 1) * rows]))
+            copies.append(put(result, out_ref, out_sems, group, pair, part))
     for copy in copies:
         copy.wait()
 
 
 def summed_kernel(inputs_ref, cotangent_ref, tokens_ref, other_ref, after_ref, out_ref, result, out_sems):
-    groups, pairs, _, rows = out_ref.shape
-    width = groups * rows
+    groups, pairs = out_ref.shape[:2]
+    width = inputs_ref.shape[1] // (2 * pairs)
     side = lax.axis_index("dp") & 1
     masked = masked_turned(cotangent_ref[...], tokens_ref[...])
     copies = []
@@ -121,8 +130,7 @@
         columns = pl.ds(pl.multiple_of((2 * pair + side) * width, 128), width)
         part = jnp.dot(masked, inputs_ref[:, columns], preferred_element_type=jnp.float32)
         for group in range(groups):
-            piece = part[:, group * rows : (group + 1) * rows] + other_ref[group, pair]
-            copies.append(put(result, out_ref, out_sems, group, pair, piece))
+            copies.append(put(result, out_ref, out_sems, group, pair, part, other_ref))
     for copy in copies:
         copy.wait()
 
@@ -131,7 +139,7 @@
     count, width = inputs.shape
     rank = cotangent.shape[1]
     pairs = width // (2 * groups * rows)
-    if rows % 128:
+    if not turned(rows):
         side = lax.axis_index("dp") & 1
         side = 1 - side if away else side
         masked = jnp.where((tokens != 0)[:, None], cotangent, jnp.bfloat16(0))
@@ -145,7 +153,7 @@
         other, _ = lax.optimization_barrier((other, after))
         return mine + other
     operands = [inputs, cotangent, tokens[None, :]]
-    result = pltpu.VMEM((groups, pairs, rank, rows), jnp.float32)
+    result = pltpu.VMEM((groups, pairs, rows // LANES * rank, LANES), jnp.float32)
     out_sems = pltpu.SemaphoreType.DMA((groups, pairs))
     if away:
         in_specs = [pl.BlockSpec(memory_space=pl.ANY)] * 3
@@ -165,7 +173,7 @@
         given_kernel if away else summed_kernel,
         in_specs=in_specs,
         out_specs=pl.BlockSpec(memory_space=pl.ANY),
-        out_shape=jax.ShapeDtypeStruct((groups, pairs, rank, rows), jnp.float32),
+        out_shape=jax.ShapeDtypeStruct((groups, pairs, rows // LANES * rank, LANES), jnp.float32),
         scratch_shapes=scratch,
         compiler_params=pltpu.CompilerParams(vmem_limit_bytes=None if away else 12 << 20),
         cost_estimate=pl.CostEstimate(
@@ -181,7 +189,7 @@
     tiles = seed_ref.shape[0] * FEAT_BLOCK // TILE_FEATS
     row = first + pl.program_id(0) // tiles * count
     start = step_start(rows, rank, groups, row // KEPT_ROWS)
-    start += row % KEPT_ROWS // minor_size(rows, rank) * strides(rows, rank)[0]
+    start += row % KEPT_ROWS // LANES * strides(rows, rank)[0]
     base = hash_base(seed_ref, pl.program_id(0) % tiles, start, strides(rows, rank)[1])
     write_signs(base, rows, rank, 0, count, out_ref)
 
@@ -207,25 +215,27 @@
 
 
 def direction_kernel(rows, gradient_ref, first_ref, second_ref, out_ref, scale_ref, held, first, second):
-    sequences, major, minor = gradient_ref.shape
+    major, sequences, minor = held.shape
     mine = pl.ds(pl.multiple_of(lax.axis_index("groups") * rows, 8), rows)
-    turn = major != rows
-    first[...] = first_ref[mine, :].T if turn else first_ref[mine, :]
-    second[...] = second_ref[mine, :].T if turn else second_ref[mine, :]
-
-    def moments(block, largest):
-        at = pl.ds(pl.multiple_of(block * 8, 8), 8)
-        gradient = gradient_ref[:, at, :]
-        moment_one = beta_one * first[at, :][None] + (1 - beta_one) * gradient
-        moment_two = beta_two * second[at, :][None] + (1 - beta_two) * gradient * gradient
+    for moment, moment_ref, beta in ((first, first_ref, beta_one), (second, second_ref, beta_two)):
+        values = beta * moment_ref[mine, :]
+        rank = values.shape[1]
+        if not turned(rows):
+            moment[...] = values
+            continue
+        for line in range(rows // LANES):
+            moment[line * rank : (line + 1) * rank, :] = values[line * LANES : (line + 1) * LANES, :].T
+
+    def moments(row, largest):
+        gradient = gradient_ref[pl.ds(row, sequences, stride=major), :]
+        moment_one = first[pl.ds(row, 1), :] + (1 - beta_one) * gradient
+        moment_two = second[pl.ds(row, 1), :] + (1 - beta_two) * gradient * gradient
         direction = moment_one / (moment_two * lax.rsqrt(moment_two) + epsilon)
         direction = direction.astype(jnp.bfloat16).astype(jnp.float32)
-        direction = jnp.swapaxes(direction, 0, 1)
-        for row in range(8):
-            held[block * 8 + row] = direction[row]
-        return jnp.maximum(largest, jnp.max(jnp.abs(direction), axis=0))
-
-    largest = lax.fori_loop(0, major // 8, moments, jnp.zeros((sequences, minor), jnp.float32))
+        held[row] = direction
+        return jnp.maximum(largest, jnp.abs(direction))
+
+    largest = lax.fori_loop(0, major, moments, jnp.zeros((sequences, minor), jnp.float32), unroll=8)
     largest = jnp.broadcast_to(jnp.max(largest, axis=1, keepdims=True), (sequences, minor))
     scale = jnp.ones_like(largest)
     for power in (64, 32, 16, 8, 4, 2, 1):
@@ -269,7 +279,7 @@
             flops=20 * gradient.size, bytes_accessed=5 * gradient.size, transcendentals=2 * gradient.size
         ),
         name="direction",
-    )(gradient, first, second)
+    )(gradient.reshape(sequences * major, minor), first, second)
 
 
 def project_kernel(rows, groups, rank, final_scale, seed_ref, direction_ref, scale_ref, kept_ref, out_ref, total, *tiles):
@@ -321,8 +331,8 @@
         grid=(features // TILE_FEATS, steps),
         in_specs=[
             pl.BlockSpec(memory_space=pltpu.SMEM),
-            pl.BlockSpec((DIGITS * sequences, params), lambda tile, step: (0, 0)),
-            pl.BlockSpec(scale.shape, lambda tile, step: (0, 0)),
+            pl.BlockSpec(memory_space=pltpu.VMEM),
+            pl.BlockSpec(memory_space=pltpu.VMEM),
             pl.BlockSpec((KEPT_ROWS, TILE_FEATS), lambda tile, step: (step, tile)),
         ],
         out_specs=pl.BlockSpec((sequences, 1, 1, TILE_FEATS), lambda tile, step: (0, tile, 0, 0)),
@@ -351,7 +361,7 @@
     rows = adam_first_moment.shape[0] // groups
     half = device_list // 2
     kept_rows = rows * rank // STEP_ROWS * KEPT_ROWS
-    early = min(EARLY_ROWS, kept_rows // 3)
+    early = min(EARLY_ROWS, kept_rows // 2)
     held = (rank_cotangent, token_identifiers)
 
     given = half_gradient(hidden_input_rows, *held, True, groups, rows)

time: 190 us -> 190 us (level)
  no operation moved by 1% of the time
where the time goes in v8:
time: 190 us
  Pallas kernels  165 us (87%)
  blocking collectives  16 us (8%)
  starting transfers between devices  8.5 us (4%)
    pallas_call x1, Pallas kernels, project(): pl.pallas_call(functools.partial(project_kernel, rows, groups, rank, fina...  95.9 us
    pallas_call x2, Pallas kernels, kept_signs(): pl.pallas_call(functools.partial(signs_kernel, rows, groups, rank, first)...  60 us
    all_to_all x1, blocking collectives, local(): lax.all_to_all(partial, ('groups', 'dp'), split_axis=0, concat_axis=0, ti...  16 us
    all_to_all x1, starting transfers between devices, local(): lax.all_to_all(summed, ('groups', 'dp'), split_axis=0, concat_axis=0, axi...  7.94 us
    pallas_call x2, Pallas kernels, half_gradient(): pl.pallas_call(given_kernel if away else summed_kernel, in_specs=in_specs...  5.27 us
  transfers between devices with their start and end apart: 2, of which 0 were waited for; matrix products, arithmetic and copies ran while one was open for 0% of the time, Pallas kernels for 32%

profile of v8, /device:TPU:0, one launch (start us, length us, event | category | flops | bytes accessed | tf_op | source)
XLA Modules:
  0.0 190.3 jit_solution(7473573429708837286)
XLA Ops:
  0.0 0.0 copy-start.4
  0.0 3.5 %half_gradient.2 = f32[2,8,256,128]{3,2,1,0:T(8,128)} custom-call(bf16[256,8192]{1,0:T(8,128)(2,1)} %inputs_ref.3, bf16[256,128]{1,0:T(8,128)(2,1)} %cotangent_ref.3, s32[1,256]{1,0:T(1,128)} %bitcast.7), custom_call_target="tpu_custom_call" | custom-call | flops 268435456 | bytes 6291456 | tf_op jit(solution)/shard_map/half_gradient/pallas_call | solution.py:172
  3.5 0.0 copy-start.1
  3.6 0.0 copy-start.5
  3.6 0.6 collective-permute-start
  4.1 0.0 copy-done.4
  4.1 0.0 copy-start
  4.1 5.1 %kept_signs.2.after_ref.refs_0_ = f8e4m3fn[12288,4096]{1,0:T(32,128)(4,1)} custom-call(s32[8]{0:T(128)S(1)} %copy-done.4), custom_call_target="tpu_custom_call" | custom-call | flops 31457280 | bytes 3145728 | tf_op jit(solution)/shard_map/kept_signs/pallas_call | solution.py:201
  9.2 0.0 collective-permute-done.other_ref
  9.2 0.0 copy-done.1
  9.2 0.0 copy-done.5
  9.2 0.0 copy-done
  9.3 1.7 half_gradient.3
  11.0 7.9 %all-to-all-start = ((f32[16,256,128]{2,1,0:T(8,128)}), f32[16,256,128]{2,1,0:T(8,128)S(1)}, u32[]{:S(2)}, u32[]{:S(2)}) async-start(f32[16,256,128]{2,1,0:T(8,128)} %bitcast.1), calls=%async_computation | async-start | bytes 4194304 | tf_op jit(solution)/shard_map/all_to_all | solution.py:377
  18.9 0.0 copy-start.2
  19.0 0.0 copy-start.3
  19.0 54.9 %kept_signs.3.kept_ref = f8e4m3fn[12288,4096]{1,0:T(32,128)(4,1)} custom-call(s32[8]{0:T(128)S(1)} %copy-done.4, f8e4m3fn[12288,4096]{1,0:T(32,128)(4,1)} %kept_signs.2.after_ref.refs_0_), custom_call_target="tpu_custom_call", output_to_operand_aliasing={{}: (1, {})} | custom-call | flops 471859200 | bytes 47185920 | tf_op jit(solution)/shard_map/kept_signs/pallas_call | solution.py:201
  73.9 0.0 all-to-all-done
  73.9 0.0 copy-done.2
  73.9 0.0 copy-done.3
  73.9 3.7 %direction.1 = (f8e4m3fn[64,32768]{1,0:T(32,128)(4,1)S(1)}, f32[16,128]{1,0:T(8,128)S(1)}) custom-call(f32[4096,128]{1,0:T(8,128)S(1)} %bitcast.5, f32[512,128]{1,0:T(8,128)S(1)} %copy-done.2, f32[512,128]{1,0:T(8,128)S(1)} %copy-done.3), custom_call_target="tpu_custom_call" | custom-call | flops 10485760 | bytes 2621440 | tf_op jit(solution)/shard_map/direction/pallas_call | solution.py:266
  77.6 95.9 %project.1 = f32[16,2,1,2048]{3,2,1,0:T(1,128)S(1)} custom-call(s32[8]{0:T(128)S(1)} %copy-done.4, f8e4m3fn[64,32768]{1,0:T(32,128)(4,1)S(1)} %get-tuple-element.7.direction_ref, f32[16,128]{1,0:T(8,128)S(1)} %get-tuple-element.8.scale_ref, f8e4m3fn[12288,4096]{1,0:T(32,128)(4,1)} %kept_signs.3.kept_ref), custom_call_target="tpu_custom_call" | custom-call | flops 1342177280 | bytes 33554432 | tf_op jit(solution)/shard_map/project/pallas_call | solution.py:329
  173.6 16.0 %all_to_all.10 = f32[32,1,2048]{2,1,0:T(1,128)S(1)} all-to-all(f32[32,1,2048]{2,1,0:T(1,128)S(1)} %bitcast.6), channel_id=1, replica_groups=mesh['groups'=2,'dp'=16] {'groups','dp'}, dimensions={0} | all-to-all | bytes 524288 | tf_op jit(solution)/shard_map/all_to_all | solution.py:385
  189.5 0.8 reduce_sum.11
Async XLA Ops:
  0.0 4.1 %copy-start.4 = (s32[8]{0:T(128)S(1)}, s32[8]{0:T(128)}, u32[]{:S(2)}) copy-start(s32[8]{0:T(128)} %seed_ref.5) | copy-start | bytes 100
  3.5 5.7 %copy-start.1 = (bf16[256,128]{1,0:T(8,128)(2,1)S(1)}, bf16[256,128]{1,0:T(8,128)(2,1)}, u32[]{:S(2)}) copy-start(bf16[256,128]{1,0:T(8,128)(2,1)} %cotangent_ref.3) | copy-start | bytes 196612
  3.6 5.7 %copy-start.5 = (s32[256]{0:T(256)S(1)}, s32[256]{0:T(256)}, u32[]{:S(2)}) copy-start(s32[256]{0:T(256)} %param.8) | copy-start | bytes 3076
  3.6 5.7 %collective-permute-start = (f32[2,8,256,128]{3,2,1,0:T(8,128)}, f32[2,8,256,128]{3,2,1,0:T(8,128)S(1)}, u32[]{:S(2)}, u32[]{:S(2)}) collective-permute-start(f32[2,8,256,128]{3,2,1,0:T(8,128)} %half_gradient.2), channel_id=1, source_target_pairs={{0,1},{1,0},{2,3},{3,2},{4,5},{5,4},{6,7},{7,6},{8,9},{9,8},{10,11... | collective-permute-start | bytes 6291464 | tf_op jit(solution)/shard_map/ppermute | solution.py:369
  4.1 5.1 %copy-start = (bf16[256,8192]{1,0:T(8,128)(2,1)S(1)}, bf16[256,8192]{1,0:T(8,128)(2,1)}, u32[]{:S(2)}) copy-start(bf16[256,8192]{1,0:T(8,128)(2,1)} %inputs_ref.3) | copy-start | bytes 12582916
  11.0 62.9 %all-to-all-start = ((f32[16,256,128]{2,1,0:T(8,128)}), f32[16,256,128]{2,1,0:T(8,128)S(1)}, u32[]{:S(2)}, u32[]{:S(2)}) async-start(f32[16,256,128]{2,1,0:T(8,128)} %bitcast.1), calls=%async_computation | async-start | bytes 4194304 | tf_op jit(solution)/shard_map/all_to_all | solution.py:377
  18.9 55.0 %copy-start.2 = (f32[512,128]{1,0:T(8,128)S(1)}, f32[512,128]{1,0:T(8,128)}, u32[]{:S(2)}) copy-start(f32[512,128]{1,0:T(8,128)} %first_ref.1) | copy-start | bytes 786436
  19.0 54.9 %copy-start.3 = (f32[512,128]{1,0:T(8,128)S(1)}, f32[512,128]{1,0:T(8,128)}, u32[]{:S(2)}) copy-start(f32[512,128]{1,0:T(8,128)} %second_ref.1) | copy-start | bytes 786436

commit v9 on v7

--- a/solution.py
+++ b/solution.py
@@ -222,10 +222,10 @@
         direction = direction.astype(jnp.bfloat16).astype(jnp.float32)
         direction = jnp.swapaxes(direction, 0, 1)
         for row in range(8):
-            held[block * 8 + row] = direction[row]
+            held[block * 8 + row] = direction[row].astype(jnp.bfloat16)
         return jnp.maximum(largest, jnp.max(jnp.abs(direction), axis=0))
 
-    largest = lax.fori_loop(0, major // 8, moments, jnp.zeros((sequences, minor), jnp.float32))
+    largest = lax.fori_loop(0, major // 8, moments, jnp.zeros((sequences, minor), jnp.float32), unroll=4)
     largest = jnp.broadcast_to(jnp.max(largest, axis=1, keepdims=True), (sequences, minor))
     scale = jnp.ones_like(largest)
     for power in (64, 32, 16, 8, 4, 2, 1):
@@ -238,17 +238,20 @@
         scale = jnp.where(over, scale * (0.5**power), scale)
     scale_ref[...] = scale
 
+    narrow = scale.astype(jnp.bfloat16)
+    radix, shift = jnp.bfloat16(RADIX), jnp.bfloat16(192.0)
+
     def split(row, _):
-        rest = held[row] * scale
+        rest = held[row] * narrow
         digits = []
         for _ in range(DIGITS):
-            digit = jnp.round(rest)
+            digit = (rest + shift) - shift
             digits.append(digit)
-            rest = (rest - digit) * RADIX
+            rest = (rest - digit) * radix
         out_ref[:, pl.ds(pl.multiple_of(row * minor, minor), minor)] = jnp.concatenate(digits, axis=0).astype(FP8)
         return 0
 
-    lax.fori_loop(0, major, split, 0, unroll=8)
+    lax.fori_loop(0, major, split, 0, unroll=64)
 
 
 def scaled_direction(gradient, first, second, rows):
@@ -260,7 +263,7 @@
             jax.ShapeDtypeStruct((sequences, minor), jnp.float32),
         ),
         scratch_shapes=[
-            pltpu.VMEM((major, sequences, minor), jnp.float32),
+            pltpu.VMEM((major, sequences, minor), jnp.bfloat16),
             pltpu.VMEM((major, minor), jnp.float32),
             pltpu.VMEM((major, minor), jnp.float32),
         ],

time: 190 us -> 189 us (level)
  no operation moved by 1% of the time
where the time goes in v9:
time: 189 us
  Pallas kernels  164 us (87%)
  blocking collectives  16 us (8%)
  starting transfers between devices  8.5 us (4%)
    pallas_call x1, Pallas kernels, project(): pl.pallas_call(functools.partial(project_kernel, rows, groups, rank, fina...  95.8 us
    pallas_call x2, Pallas kernels, kept_signs(): pl.pallas_call(functools.partial(signs_kernel, rows, groups, rank, first)...  60.5 us
    all_to_all x1, blocking collectives, local(): lax.all_to_all(partial, ('groups', 'dp'), split_axis=0, concat_axis=0, ti...  16 us
    all_to_all x1, starting transfers between devices, local(): lax.all_to_all(summed, ('groups', 'dp'), split_axis=0, concat_axis=0, axi...  7.94 us
    pallas_call x2, Pallas kernels, half_gradient(): pl.pallas_call(given_kernel if away else summed_kernel, in_specs=in_specs...  5.26 us
  transfers between devices with their start and end apart: 2, of which 0 were waited for; matrix products, arithmetic and copies ran while one was open for 0% of the time, Pallas kernels for 32%

profile of v9, /device:TPU:0, one launch (start us, length us, event | category | flops | bytes accessed | tf_op | source)
XLA Modules:
  0.0 189.3 jit_solution(676698470286695947)
XLA Ops:
  0.0 0.0 copy-start.4
  0.0 3.5 %half_gradient.2 = f32[2,8,128,256]{3,2,1,0:T(8,128)} custom-call(bf16[256,8192]{1,0:T(8,128)(2,1)} %inputs_ref.3, bf16[256,128]{1,0:T(8,128)(2,1)} %cotangent_ref.3, s32[1,256]{1,0:T(1,128)} %bitcast.5), custom_call_target="tpu_custom_call" | custom-call | flops 268435456 | bytes 6291456 | tf_op jit(solution)/shard_map/half_gradient/pallas_call | solution.py:164
  3.5 0.0 copy-start.1
  3.6 0.0 copy-start.5
  3.6 0.6 collective-permute-start
  4.1 0.0 copy-done.4
  4.1 0.0 copy-start
  4.1 6.3 %kept_signs.2.after_ref.refs_0_ = f8e4m3fn[12288,4096]{1,0:T(32,128)(4,1)} custom-call(s32[8]{0:T(128)S(1)} %copy-done.4), custom_call_target="tpu_custom_call" | custom-call | flops 41943040 | bytes 4194304 | tf_op jit(solution)/shard_map/kept_signs/pallas_call | solution.py:193
  10.4 0.0 collective-permute-done.other_ref
  10.4 0.0 copy-done.1
  10.4 0.0 copy-done.5
  10.4 0.0 copy-done
  10.4 1.7 half_gradient.3
  12.1 7.9 %all-to-all-start = ((f32[16,128,256]{2,1,0:T(8,128)}), f32[16,128,256]{2,1,0:T(8,128)S(1)}, u32[]{:S(2)}, u32[]{:S(2)}) async-start(f32[16,128,256]{2,1,0:T(8,128)} %bitcast.1), calls=%async_computation | async-start | bytes 4194304 | tf_op jit(solution)/shard_map/all_to_all | solution.py:370
  20.1 0.0 copy-start.2
  20.1 0.0 copy-start.3
  20.1 54.3 %kept_signs.3.kept_ref = f8e4m3fn[12288,4096]{1,0:T(32,128)(4,1)} custom-call(s32[8]{0:T(128)S(1)} %copy-done.4, f8e4m3fn[12288,4096]{1,0:T(32,128)(4,1)} %kept_signs.2.after_ref.refs_0_), custom_call_target="tpu_custom_call", output_to_operand_aliasing={{}: (1, {})} | custom-call | flops 461373440 | bytes 46137344 | tf_op jit(solution)/shard_map/kept_signs/pallas_call | solution.py:193
  74.4 0.0 all-to-all-done.gradient_ref
  74.4 0.0 copy-done.2
  74.4 0.0 copy-done.3
  74.4 2.4 %direction.1 = (f8e4m3fn[64,32768]{1,0:T(32,128)(4,1)S(1)}, f32[16,256]{1,0:T(8,128)S(1)}) custom-call(f32[16,128,256]{2,1,0:T(8,128)S(1)} %all-to-all-done.gradient_ref, f32[512,128]{1,0:T(8,128)S(1)} %copy-done.2, f32[512,128]{1,0:T(8,128)S(1)} %copy-done.3), custom_call_target="tpu_custom_call" | custom-call | flops 10485760 | bytes 2621440 | tf_op jit(solution)/shard_map/direction/pallas_call | solution.py:259
  76.7 95.8 %project.1 = f32[16,2,1,2048]{3,2,1,0:T(1,128)S(1)} custom-call(s32[8]{0:T(128)S(1)} %copy-done.4, f8e4m3fn[64,32768]{1,0:T(32,128)(4,1)S(1)} %get-tuple-element.7.direction_ref, f32[16,256]{1,0:T(8,128)S(1)} %get-tuple-element.8.scale_ref, f8e4m3fn[12288,4096]{1,0:T(32,128)(4,1)} %kept_signs.3.kept_ref), custom_call_target="tpu_custom_call" | custom-call | flops 1342177280 | bytes 33554432 | tf_op jit(solution)/shard_map/project/pallas_call | solution.py:322
  172.6 16.0 %all_to_all.10 = f32[32,1,2048]{2,1,0:T(1,128)S(1)} all-to-all(f32[32,1,2048]{2,1,0:T(1,128)S(1)} %bitcast.4), channel_id=1, replica_groups=mesh['groups'=2,'dp'=16] {'groups','dp'}, dimensions={0} | all-to-all | bytes 524288 | tf_op jit(solution)/shard_map/all_to_all | solution.py:378
  188.5 0.8 reduce_sum.11
Async XLA Ops:
  0.0 4.1 %copy-start.4 = (s32[8]{0:T(128)S(1)}, s32[8]{0:T(128)}, u32[]{:S(2)}) copy-start(s32[8]{0:T(128)} %seed_ref.5) | copy-start | bytes 100
  3.5 6.8 %copy-start.1 = (bf16[256,128]{1,0:T(8,128)(2,1)S(1)}, bf16[256,128]{1,0:T(8,128)(2,1)}, u32[]{:S(2)}) copy-start(bf16[256,128]{1,0:T(8,128)(2,1)} %cotangent_ref.3) | copy-start | bytes 196612
  3.6 6.8 %copy-start.5 = (s32[256]{0:T(256)S(1)}, s32[256]{0:T(256)}, u32[]{:S(2)}) copy-start(s32[256]{0:T(256)} %param.8) | copy-start | bytes 3076
  3.6 6.8 %collective-permute-start = (f32[2,8,128,256]{3,2,1,0:T(8,128)}, f32[2,8,128,256]{3,2,1,0:T(8,128)S(1)}, u32[]{:S(2)}, u32[]{:S(2)}) collective-permute-start(f32[2,8,128,256]{3,2,1,0:T(8,128)} %half_gradient.2), channel_id=1, source_target_pairs={{0,1},{1,0},{2,3},{3,2},{4,5},{5,4},{6,7},{7,6},{8,9},{9,8},{10,11... | collective-permute-start | bytes 6291464 | tf_op jit(solution)/shard_map/ppermute | solution.py:362
  4.1 6.3 %copy-start = (bf16[256,8192]{1,0:T(8,128)(2,1)S(1)}, bf16[256,8192]{1,0:T(8,128)(2,1)}, u32[]{:S(2)}) copy-start(bf16[256,8192]{1,0:T(8,128)(2,1)} %inputs_ref.3) | copy-start | bytes 12582916
  12.1 62.2 %all-to-all-start = ((f32[16,128,256]{2,1,0:T(8,128)}), f32[16,128,256]{2,1,0:T(8,128)S(1)}, u32[]{:S(2)}, u32[]{:S(2)}) async-start(f32[16,128,256]{2,1,0:T(8,128)} %bitcast.1), calls=%async_computation | async-start | bytes 4194304 | tf_op jit(solution)/shard_map/all_to_all | solution.py:370
  20.1 54.3 %copy-start.2 = (f32[512,128]{1,0:T(8,128)S(1)}, f32[512,128]{1,0:T(8,128)}, u32[]{:S(2)}) copy-start(f32[512,128]{1,0:T(8,128)} %first_ref.1) | copy-start | bytes 786436
  20.1 54.3 %copy-start.3 = (f32[512,128]{1,0:T(8,128)S(1)}, f32[512,128]{1,0:T(8,128)}, u32[]{:S(2)}) copy-start(f32[512,128]{1,0:T(8,128)} %second_ref.1) | copy-start | bytes 786436

commit v10 on v9

--- a/solution.py
+++ b/solution.py
@@ -20,7 +20,7 @@
 FP8 = jnp.float8_e4m3fn
 STEP_ROWS = 4096
 KEPT_ROWS = 1536
-TILES = (1280, 1024, 256)
+TILES = (2304, 256)
 EARLY_ROWS, EARLY_BLOCK = 1024, 512
 LATER_BLOCK = 512
 TILE_FEATS = 2048

time: 189 us -> 189 us (level)
  no operation moved by 1% of the time
where the time goes in v10:
time: 189 us
  Pallas kernels  164 us (87%)
  blocking collectives  16 us (8%)
  starting transfers between devices  8.5 us (4%)
    pallas_call x1, Pallas kernels, project(): pl.pallas_call(functools.partial(project_kernel, rows, groups, rank, fina...  95.7 us
    pallas_call x2, Pallas kernels, kept_signs(): pl.pallas_call(functools.partial(signs_kernel, rows, groups, rank, first)...  60.5 us
    all_to_all x1, blocking collectives, local(): lax.all_to_all(partial, ('groups', 'dp'), split_axis=0, concat_axis=0, ti...  16 us
    all_to_all x1, starting transfers between devices, local(): lax.all_to_all(summed, ('groups', 'dp'), split_axis=0, concat_axis=0, axi...  7.94 us
    pallas_call x2, Pallas kernels, half_gradient(): pl.pallas_call(given_kernel if away else summed_kernel, in_specs=in_specs...  5.26 us
  transfers between devices with their start and end apart: 2, of which 0 were waited for; matrix products, arithmetic and copies ran while one was open for 0% of the time, Pallas kernels for 32%

profile of v10, /device:TPU:0, one launch (start us, length us, event | category | flops | bytes accessed | tf_op | source)
XLA Modules:
  0.0 189.2 jit_solution(15183104912923646414)
XLA Ops:
  0.0 0.0 copy-start.4
  0.0 3.5 %half_gradient.2 = f32[2,8,128,256]{3,2,1,0:T(8,128)} custom-call(bf16[256,8192]{1,0:T(8,128)(2,1)} %inputs_ref.3, bf16[256,128]{1,0:T(8,128)(2,1)} %cotangent_ref.3, s32[1,256]{1,0:T(1,128)} %bitcast.5), custom_call_target="tpu_custom_call" | custom-call | flops 268435456 | bytes 6291456 | tf_op jit(solution)/shard_map/half_gradient/pallas_call | solution.py:164
  3.5 0.0 copy-start.1
  3.6 0.0 copy-start.5
  3.6 0.6 collective-permute-start
  4.1 0.0 copy-done.4
  4.1 0.0 copy-start
  4.1 6.3 %kept_signs.2.after_ref.refs_0_ = f8e4m3fn[12288,4096]{1,0:T(32,128)(4,1)} custom-call(s32[8]{0:T(128)S(1)} %copy-done.4), custom_call_target="tpu_custom_call" | custom-call | flops 41943040 | bytes 4194304 | tf_op jit(solution)/shard_map/kept_signs/pallas_call | solution.py:193
  10.4 0.0 collective-permute-done.other_ref
  10.4 0.0 copy-done.1
  10.4 0.0 copy-done.5
  10.4 0.0 copy-done
  10.4 1.7 half_gradient.3
  12.1 7.9 %all-to-all-start = ((f32[16,128,256]{2,1,0:T(8,128)}), f32[16,128,256]{2,1,0:T(8,128)S(1)}, u32[]{:S(2)}, u32[]{:S(2)}) async-start(f32[16,128,256]{2,1,0:T(8,128)} %bitcast.1), calls=%async_computation | async-start | bytes 4194304 | tf_op jit(solution)/shard_map/all_to_all | solution.py:370
  20.1 0.0 copy-start.2
  20.1 0.0 copy-start.3
  20.1 54.3 %kept_signs.3.kept_ref = f8e4m3fn[12288,4096]{1,0:T(32,128)(4,1)} custom-call(s32[8]{0:T(128)S(1)} %copy-done.4, f8e4m3fn[12288,4096]{1,0:T(32,128)(4,1)} %kept_signs.2.after_ref.refs_0_), custom_call_target="tpu_custom_call", output_to_operand_aliasing={{}: (1, {})} | custom-call | flops 461373440 | bytes 46137344 | tf_op jit(solution)/shard_map/kept_signs/pallas_call | solution.py:193
  74.4 0.0 all-to-all-done.gradient_ref
  74.4 0.0 copy-done.2
  74.4 0.0 copy-done.3
  74.4 2.4 %direction.1 = (f8e4m3fn[64,32768]{1,0:T(32,128)(4,1)S(1)}, f32[16,256]{1,0:T(8,128)S(1)}) custom-call(f32[16,128,256]{2,1,0:T(8,128)S(1)} %all-to-all-done.gradient_ref, f32[512,128]{1,0:T(8,128)S(1)} %copy-done.2, f32[512,128]{1,0:T(8,128)S(1)} %copy-done.3), custom_call_target="tpu_custom_call" | custom-call | flops 10485760 | bytes 2621440 | tf_op jit(solution)/shard_map/direction/pallas_call | solution.py:259
  76.7 95.7 %project.1 = f32[16,2,1,2048]{3,2,1,0:T(1,128)S(1)} custom-call(s32[8]{0:T(128)S(1)} %copy-done.4, f8e4m3fn[64,32768]{1,0:T(32,128)(4,1)S(1)} %get-tuple-element.7.direction_ref, f32[16,256]{1,0:T(8,128)S(1)} %get-tuple-element.8.scale_ref, f8e4m3fn[12288,4096]{1,0:T(32,128)(4,1)} %kept_signs.3.kept_ref), custom_call_target="tpu_custom_call" | custom-call | flops 1342177280 | bytes 33554432 | tf_op jit(solution)/shard_map/project/pallas_call | solution.py:322
  172.5 16.0 %all_to_all.10 = f32[32,1,2048]{2,1,0:T(1,128)S(1)} all-to-all(f32[32,1,2048]{2,1,0:T(1,128)S(1)} %bitcast.4), channel_id=1, replica_groups=mesh['groups'=2,'dp'=16] {'groups','dp'}, dimensions={0} | all-to-all | bytes 524288 | tf_op jit(solution)/shard_map/all_to_all | solution.py:378
  188.4 0.8 reduce_sum.11
Async XLA Ops:
  0.0 4.1 %copy-start.4 = (s32[8]{0:T(128)S(1)}, s32[8]{0:T(128)}, u32[]{:S(2)}) copy-start(s32[8]{0:T(128)} %seed_ref.5) | copy-start | bytes 100
  3.5 6.8 %copy-start.1 = (bf16[256,128]{1,0:T(8,128)(2,1)S(1)}, bf16[256,128]{1,0:T(8,128)(2,1)}, u32[]{:S(2)}) copy-start(bf16[256,128]{1,0:T(8,128)(2,1)} %cotangent_ref.3) | copy-start | bytes 196612
  3.6 6.8 %copy-start.5 = (s32[256]{0:T(256)S(1)}, s32[256]{0:T(256)}, u32[]{:S(2)}) copy-start(s32[256]{0:T(256)} %param.8) | copy-start | bytes 3076
  3.6 6.8 %collective-permute-start = (f32[2,8,128,256]{3,2,1,0:T(8,128)}, f32[2,8,128,256]{3,2,1,0:T(8,128)S(1)}, u32[]{:S(2)}, u32[]{:S(2)}) collective-permute-start(f32[2,8,128,256]{3,2,1,0:T(8,128)} %half_gradient.2), channel_id=1, source_target_pairs={{0,1},{1,0},{2,3},{3,2},{4,5},{5,4},{6,7},{7,6},{8,9},{9,8},{10,11... | collective-permute-start | bytes 6291464 | tf_op jit(solution)/shard_map/ppermute | solution.py:362
  4.1 6.3 %copy-start = (bf16[256,8192]{1,0:T(8,128)(2,1)S(1)}, bf16[256,8192]{1,0:T(8,128)(2,1)}, u32[]{:S(2)}) copy-start(bf16[256,8192]{1,0:T(8,128)(2,1)} %inputs_ref.3) | copy-start | bytes 12582916
  12.1 62.2 %all-to-all-start = ((f32[16,128,256]{2,1,0:T(8,128)}), f32[16,128,256]{2,1,0:T(8,128)S(1)}, u32[]{:S(2)}, u32[]{:S(2)}) async-start(f32[16,128,256]{2,1,0:T(8,128)} %bitcast.1), calls=%async_computation | async-start | bytes 4194304 | tf_op jit(solution)/shard_map/all_to_all | solution.py:370
  20.1 54.3 %copy-start.2 = (f32[512,128]{1,0:T(8,128)S(1)}, f32[512,128]{1,0:T(8,128)}, u32[]{:S(2)}) copy-start(f32[512,128]{1,0:T(8,128)} %first_ref.1) | copy-start | bytes 786436
  20.1 54.3 %copy-start.3 = (f32[512,128]{1,0:T(8,128)S(1)}, f32[512,128]{1,0:T(8,128)}, u32[]{:S(2)}) copy-start(f32[512,128]{1,0:T(8,128)} %second_ref.1) | copy-start | bytes 786436
